TPU v7x, 128 devices: a whole 4x4x4 slice. The times are simulated.
128 devices in a mesh: row: 16 (over y_hi, x, core), col: 8 (over y_lo, z).
Axes of the slice: x: 4, y: 4 (y_hi: 2, y_lo: 2; y = y_hi * 2 + y_lo), z: 4, core: 2. Of those that a mesh axis runs over, the one named last changes fastest.
Arguments:
- pair_activation: bfloat16 [1024, 1024, 128], P('row', 'col'), may hold values from -80 to 80
- target_distance_bins: int32 [1024, 1024], P('row', 'col'), may hold values from 0 to 63, as said below
- distogram_weight: bfloat16 [128, 64], replicated, may hold values from -2 to 2
- distogram_bias: float32 [64], replicated, may hold values from -0.25 to 0.25
- outer_pair_weight: bfloat16 [1024, 128], replicated, may hold values from -0.1875 to 0.1875
- stored_lhs_operand: bfloat16 [256, 32, 1024], P('row', None, 'col'), may hold values from -6 to 6
- stored_rhs_operand: bfloat16 [256, 32, 1024], P('row', None, 'col'), may hold values from -6 to 6
- left_projection_weight: bfloat16 [64, 32], replicated, may hold values from -0.75 to 0.75
- right_projection_weight: bfloat16 [64, 32], replicated, may hold values from -0.75 to 0.75
- outer_mean_norm_gain: float32 [64], replicated, may hold values from 0.25 to 1.75
- transition_norm_gain: float32 [64], replicated, may hold values from 0.25 to 1.75
- gate_weight: bfloat16 [64, 256], replicated, may hold values from -0.75 to 0.75
- up_weight: bfloat16 [64, 256], replicated, may hold values from -0.75 to 0.75
- down_weight: bfloat16 [256, 64], replicated, may hold values from -0.375 to 0.375
- side_stack_entry: bfloat16 [256, 64, 1024], P(('row', 'col')), may hold values from -6 to 6
- arriving_stack_derivative: bfloat16 [256, 64, 1024], P(('row', 'col')), may hold values from -4 to 4
Outputs:
- pair_activation_gradient: bfloat16 [1024, 1024, 128], P('row', 'col')
- alignment_gradient: bfloat16 [256, 64, 1024], P(('row', 'col'))
Inputs may be any that keep to these rules, and one draw needn't show every extreme that they name: target_distance_bins[i, j] equals target_distance_bins[j, i].
All inputs are finite; a program needn't handle non-finite values.
Results may differ from a plain program's by a relative error of at most 0.0098.
Values may be sent and summed in bfloat16 or wider, within the bound.
A program may use at most 64 MiB of HBM per device.

v0:
```python
import jax
import jax.numpy as jnp
from jax import lax
from jax.sharding import PartitionSpec as P


def apply_layer_norm(features):
    centered = features - jnp.mean(features, axis=1, keepdims=True)
    scale_inv = lax.rsqrt(jnp.mean(centered * centered, axis=1, keepdims=True) + 1e-05)
    return (centered * scale_inv, scale_inv)


def norm_backward_step(incoming, normed_field, scale_inv):
    first_mean = jnp.mean(incoming, axis=1, keepdims=True)
    second_mean = jnp.mean(incoming * normed_field, axis=1, keepdims=True)
    return scale_inv * (incoming - first_mean - normed_field * second_mean)


def regroup(logit_tile):
    return lax.all_to_all(logit_tile, "col", split_axis=1, concat_axis=2, tiled=True)


def per_device(
    pair_activation,
    target_distance_bins,
    distogram_weight,
    distogram_bias,
    outer_pair_weight,
    stored_lhs_operand,
    stored_rhs_operand,
    left_projection_weight,
    right_projection_weight,
    outer_mean_norm_gain,
    transition_norm_gain,
    gate_weight,
    up_weight,
    down_weight,
    side_stack_entry,
    arriving_stack_derivative,
):
    pair_rows = pair_activation.shape[0]
    pair_cols = pair_activation.shape[1]
    bin_count = distogram_weight.shape[1]
    factor_width = stored_lhs_operand.shape[1]
    row_devices = lax.axis_size("row")
    seq_total = stored_lhs_operand.shape[0] * row_devices
    alignment_widened = side_stack_entry.astype(jnp.float32)
    first_normed_rows, first_inverse_scale = apply_layer_norm(alignment_widened)
    normed_input = (first_normed_rows * transition_norm_gain[None, :, None]).astype(jnp.bfloat16)
    gate_value = jnp.einsum(
        "smi,mh->shi", normed_input, gate_weight, preferred_element_type=jnp.float32
    )
    upward = jnp.einsum("smi,mh->shi", normed_input, up_weight, preferred_element_type=jnp.float32)
    hidden_state = (jax.nn.silu(gate_value) * upward).astype(jnp.bfloat16)
    alignment_output = alignment_widened + jnp.einsum(
        "ajc,jr->arc", hidden_state, down_weight, preferred_element_type=jnp.float32
    )
    second_normed_rows, second_inverse_scale = apply_layer_norm(alignment_output)
    logits = jnp.einsum(
        "ijp,pb->bij", pair_activation, distogram_weight, preferred_element_type=jnp.float32
    )
    logits = (logits + distogram_bias[:, None, None]).astype(jnp.bfloat16)
    flipped = lax.all_to_all(
        regroup(logits), ("row", "col"), split_axis=2, concat_axis=1, tiled=True
    )
    mirrored = jnp.swapaxes(regroup(flipped), 1, 2)
    symmetric = logits.astype(jnp.float32) + mirrored.astype(jnp.float32)
    probability = jax.nn.softmax(symmetric, axis=0)
    bin_levels = lax.broadcasted_iota(jnp.int32, (bin_count, 1, 1), 0)
    one_hot = (target_distance_bins[None, :, :] == bin_levels).astype(jnp.float32)
    logit_grad = (2.0 * (probability - one_hot)).astype(jnp.bfloat16)
    pair_activation_gradient = jnp.einsum(
        "bij,pb->ijp", logit_grad, distogram_weight, preferred_element_type=jnp.float32
    ).astype(jnp.bfloat16)
    left_all, right_all = (
        lax.all_gather(stored_lhs_operand, "row", axis=0, tiled=True),
        lax.all_gather(stored_rhs_operand, "row", axis=0, tiled=True),
    )
    seq_count = left_all.shape[0]
    step_rows = 8

    def single_tile(block_index, contribution):
        row_start = block_index * step_rows
        grad_rows = lax.dynamic_slice_in_dim(pair_activation_gradient, row_start, step_rows, 0)
        tensor_product_derivative = jnp.einsum(
            "ijp,kp->ijk", grad_rows, outer_pair_weight, preferred_element_type=jnp.float32
        ).astype(jnp.bfloat16)
        tensor_product_derivative = tensor_product_derivative.reshape(
            step_rows, pair_cols, factor_width, factor_width
        )
        lhs_portion = jnp.einsum(
            "tdpa,wad->wpt",
            tensor_product_derivative,
            right_all,
            preferred_element_type=jnp.float32,
        )
        rhs_portion = jnp.einsum(
            "ijce,scj->sei", tensor_product_derivative, left_all, preferred_element_type=jnp.float32
        )
        joined = jnp.concatenate([lhs_portion, rhs_portion], axis=1)
        return lax.dynamic_update_slice_in_dim(contribution, joined, row_start, 2)

    contribution = lax.fori_loop(
        0,
        pair_rows // step_rows,
        single_tile,
        jnp.zeros((seq_count, 2 * factor_width, pair_rows), jnp.float32),
    )
    both_weights = jnp.concatenate(
        [left_projection_weight, right_projection_weight], axis=1
    ).astype(jnp.float32)
    partial_terms = (
        jnp.einsum("mc,sci->smi", both_weights, contribution, precision=lax.Precision.HIGHEST)
        / seq_total
    )
    reduced_part = lax.psum_scatter(partial_terms, "col", scatter_dimension=2, tiled=True)
    sequence_grad = lax.all_to_all(
        reduced_part.astype(jnp.bfloat16), ("row", "col"), split_axis=0, concat_axis=2, tiled=True
    )
    norm_input_gradient = sequence_grad.astype(jnp.float32)
    middle_gradient = arriving_stack_derivative.astype(jnp.float32) + norm_backward_step(
        norm_input_gradient * outer_mean_norm_gain[None, :, None],
        second_normed_rows,
        second_inverse_scale,
    )
    mid_half = middle_gradient.astype(jnp.bfloat16)
    hidden_grad = jnp.einsum(
        "smi,hm->shi", mid_half, down_weight, preferred_element_type=jnp.float32
    )
    sigmoid_gate = jax.nn.sigmoid(gate_value)
    gate_grad = (
        hidden_grad * upward * sigmoid_gate * (1.0 + gate_value * (1.0 - sigmoid_gate))
    ).astype(jnp.bfloat16)
    up_grad = (hidden_grad * gate_value * sigmoid_gate).astype(jnp.bfloat16)
    normed_rows_gradient = jnp.einsum(
        "shi,mh->smi", gate_grad, gate_weight, preferred_element_type=jnp.float32
    )
    normed_rows_gradient = normed_rows_gradient + jnp.einsum(
        "shi,mh->smi", up_grad, up_weight, preferred_element_type=jnp.float32
    )
    alignment_gradient = middle_gradient + norm_backward_step(
        normed_rows_gradient * transition_norm_gain[None, :, None],
        first_normed_rows,
        first_inverse_scale,
    )
    return (pair_activation_gradient, alignment_gradient.astype(jnp.bfloat16))


def solution(mesh):
    return jax.shard_map(
        per_device,
        mesh=mesh,
        in_specs=(
            P("row", "col", None),
            P("row", "col"),
            P(),
            P(),
            P(),
            P("row", None, "col"),
            P("row", None, "col"),
            P(),
            P(),
            P(),
            P(),
            P(),
            P(),
            P(),
            P(("row", "col"), None, None),
            P(("row", "col"), None, None),
        ),
        out_specs=(P("row", "col", None), P(("row", "col"), None, None)),
        check_vma=False,
    )
```

profile of v0, /device:TPU:1, one launch (start us, length us, event | category | flops | bytes accessed | tf_op | source)
XLA Modules:
  0.0 323.1 jit_solution(14338661955172984682)
XLA Ops:
  12.3 22.4 %all_to_all.54 = bf16[64,64,128]{2,0,1:T(8,128)(2,1)} all-to-all(bf16[64,64,128]{2,0,1:T(8,128)(2,1)S(1)} %add_convert_fusion), channel_id=1, replica_groups=mesh['row'=16,'col'=8] {'col'}, dimensions={1} | all-to-all | bytes 2097152 | tf_op jit(solution)/shard_map/all_to_all | solution.py:20
  37.6 4.6 %reshape.88 = bf16[128,2,2048]{2,1,0:T(2,128)(2,1)} reshape(bf16[1024,8,64]{2,1,0:T(8,128)(2,1)} %bitcast.172) | data formatting | bytes 2097152
  42.2 30.8 %all_to_all.55 = bf16[128,2,2048]{2,1,0:T(2,128)(2,1)} all-to-all(bf16[128,2,2048]{2,1,0:T(2,128)(2,1)} %reshape.88), channel_id=1, replica_groups=mesh['row'=16,'col'=8] {'row','col'}, dimensions={0} | all-to-all | bytes 2097152 | tf_op jit(solution)/shard_map/all_to_all | solution.py:63
  73.1 4.8 %reshape.89 = bf16[1024,8,64]{2,1,0:T(8,128)(2,1)} reshape(bf16[128,2,2048]{2,1,0:T(2,128)(2,1)} %all_to_all.55) | data formatting | bytes 2097152
  77.8 3.6 %copy.127 = bf16[64,128,8,8]{0,3,2,1:T(8,128)(2,1)} copy(bf16[64,128,8,8]{0,2,3,1:T(8,128)(2,1)} %bitcast.174) | data formatting | bytes 2097152 | tf_op jit(solution)/shard_map/all_to_all | solution.py:63
  81.4 4.4 %reshape.90 = bf16[8,2,32768]{2,1,0:T(2,128)(2,1)} reshape(bf16[1024,8,64]{2,1,0:T(8,128)(2,1)} %bitcast.175) | data formatting | bytes 2097152
  85.7 4.2 %all-to-all-start.2 = ((bf16[8,2,32768]{2,1,0:T(2,128)(2,1)}), bf16[8,2,32768]{2,1,0:T(2,128)(2,1)}, u32[]{:S(2)}, u32[]{:S(2)}) async-start(bf16[8,2,32768]{2,1,0:T(2,128)(2,1)} %reshape.90), calls=%async_computation.2 | async-start | bytes 2097152 | tf_op jit(solution)/shard_map/all_to_all | solution.py:20
  90.4 14.5 %all-to-all-done.2 = bf16[8,2,32768]{2,1,0:T(2,128)(2,1)} async-done(((bf16[8,2,32768]{2,1,0:T(2,128)(2,1)}), bf16[8,2,32768]{2,1,0:T(2,128)(2,1)}, u32[]{:S(2)}, u32[]{:S(2)}) %all-to-all-start.2) | async-done | bytes 1048608 | tf_op jit(solution)/shard_map/all_to_all | solution.py:20
  104.9 4.3 %reshape.91 = bf16[1024,8,64]{2,1,0:T(8,128)(2,1)} reshape(bf16[8,2,32768]{2,1,0:T(2,128)(2,1)} %all-to-all-done.2) | data formatting | bytes 2097152
  109.2 4.3 %copy.128 = bf16[64,1024,8]{1,2,0:T(8,128)(2,1)} copy(bf16[64,1024,8]{0,2,1:T(8,128)(2,1)} %bitcast.173) | data formatting | bytes 2097152 | tf_op jit(solution)/shard_map/all_to_all | solution.py:20
  117.9 4.9 %convolution_convert_fusion.1 = bf16[64,128,128]{2,1,0:T(8,128)(2,1)} fusion(s32[64,128]{1,0:T(8,128)S(1)} %copy-done.28, bf16[128,64]{0,1:T(8,128)(2,1)S(1)} %copy-done.20, f32[64,64,128]{2,0,1:T(8,128)} %bitcast_add_fusion), kind=kOutput, calls=%fused_computation.37 | convolution fusion | flops 138952832 | bytes 4243456 | tf_op jit(solution)/shard_map/bij,pb->ijp/dot_general | solution.py:72
  125.3 96.9 %while.13 = (s32[]{:T(128)}, f32[256,64,64]{0,1,2:T(8,128)}, bf16[64,128,128]{2,1,0:T(8,128)(2,1)}, bf16[1024,128]{1,0:T(8,128)(2,1)S(1)}, bf16[256,32,128]{2,0,...) while((s32[]{:T(128)}, f32[256,64,64]{0,1,2:T(8,128)}, ...), condition=%wide.region_7.8_spmd, body=%wide.region_6.7_spmd.sunk | while | flops 1343356928 | bytes 33554648 | solution.py:103
  128.3 3.9 %copy.157 = bf16[8,128,1024]{1,2,0:T(8,128)(2,1)} copy(bf16[8,128,1024]{2,1,0:T(8,128)(2,1)} %convolution_convert_fusion.3) | data formatting | bytes 4194304 | tf_op jit(solution)/shard_map/while/body/eval_jaxpr/convert_element_type | solution.py:87
  140.4 3.9 %copy.157 = bf16[8,128,1024]{1,2,0:T(8,128)(2,1)} copy(bf16[8,128,1024]{2,1,0:T(8,128)(2,1)} %convolution_convert_fusion.3) | data formatting | bytes 4194304 | tf_op jit(solution)/shard_map/while/body/eval_jaxpr/convert_element_type | solution.py:87
  152.5 3.9 %copy.157 = bf16[8,128,1024]{1,2,0:T(8,128)(2,1)} copy(bf16[8,128,1024]{2,1,0:T(8,128)(2,1)} %convolution_convert_fusion.3) | data formatting | bytes 4194304 | tf_op jit(solution)/shard_map/while/body/eval_jaxpr/convert_element_type | solution.py:87
  164.7 3.9 %copy.157 = bf16[8,128,1024]{1,2,0:T(8,128)(2,1)} copy(bf16[8,128,1024]{2,1,0:T(8,128)(2,1)} %convolution_convert_fusion.3) | data formatting | bytes 4194304 | tf_op jit(solution)/shard_map/while/body/eval_jaxpr/convert_element_type | solution.py:87
  176.8 3.9 %copy.157 = bf16[8,128,1024]{1,2,0:T(8,128)(2,1)} copy(bf16[8,128,1024]{2,1,0:T(8,128)(2,1)} %convolution_convert_fusion.3) | data formatting | bytes 4194304 | tf_op jit(solution)/shard_map/while/body/eval_jaxpr/convert_element_type | solution.py:87
  188.9 3.9 %copy.157 = bf16[8,128,1024]{1,2,0:T(8,128)(2,1)} copy(bf16[8,128,1024]{2,1,0:T(8,128)(2,1)} %convolution_convert_fusion.3) | data formatting | bytes 4194304 | tf_op jit(solution)/shard_map/while/body/eval_jaxpr/convert_element_type | solution.py:87
  201.0 3.9 %copy.157 = bf16[8,128,1024]{1,2,0:T(8,128)(2,1)} copy(bf16[8,128,1024]{2,1,0:T(8,128)(2,1)} %convolution_convert_fusion.3) | data formatting | bytes 4194304 | tf_op jit(solution)/shard_map/while/body/eval_jaxpr/convert_element_type | solution.py:87
  213.1 3.9 %copy.157 = bf16[8,128,1024]{1,2,0:T(8,128)(2,1)} copy(bf16[8,128,1024]{2,1,0:T(8,128)(2,1)} %convolution_convert_fusion.3) | data formatting | bytes 4194304 | tf_op jit(solution)/shard_map/while/body/eval_jaxpr/convert_element_type | solution.py:87
  222.2 6.5 %multiply_bitcast_fusion = f32[256,64,64]{0,1,2:T(8,128)} fusion(f32[256,64,64]{0,1,2:T(8,128)} %get-tuple-element.111, bf16[64,32]{1,0:T(8,128)(2,1)S(1)} %copy.134, bf16[64,32]{1,0:T(8,128)(2,1)S(1)} %copy.133), kind=kOutput, calls=%fused_computation.14 | convolution fusion | flops 806371328 | bytes 8396800 | tf_op jit(solution)/shard_map/mc,sci->smi/dot_general | solution.py:113
  232.4 47.7 %reduce-scatter.2.cloned.1.call-done = f32[256,64,8]{0,1,2:T(8,128)} async-done(((f32[256,64,64]{0,1,2:T(8,128)}), f32[256,64,8]{0,1,2:T(8,128)}) %reduce-scatter.2.cloned.1.call-update) | async-done | bytes 524304 | tf_op jit(solution)/shard_map/reduce_scatter | solution.py:116
  284.2 7.5 %all-to-all-start.3 = ((bf16[128,2,512]{2,1,0:T(2,128)(2,1)}), bf16[128,2,512]{2,1,0:T(2,128)(2,1)}, u32[]{:S(2)}, u32[]{:S(2)}) async-start(bf16[128,2,512]{2,1,0:T(2,128)(2,1)} %reshape.92), calls=%async_computation.4 | async-start | bytes 524288 | tf_op jit(solution)/shard_map/all_to_all | solution.py:117
  291.8 10.5 %all-to-all-done.3 = bf16[128,2,512]{2,1,0:T(2,128)(2,1)} async-done(((bf16[128,2,512]{2,1,0:T(2,128)(2,1)}), bf16[128,2,512]{2,1,0:T(2,128)(2,1)}, u32[]{:S(2)}, u32[]{:S(2)}) %all-to-all-start.3) | async-done | bytes 262176 | tf_op jit(solution)/shard_map/all_to_all | solution.py:117
  (163 shorter events, 102.5 us)
Async XLA Ops:
  7.2 3.5 %copy-start = (bf16[64,128,128]{2,1,0:T(8,128)(2,1)S(1)}, bf16[64,128,128]{2,1,0:T(8,128)(2,1)}, u32[]{:S(2)}) copy-start(bf16[64,128,128]{2,1,0:T(8,128)(2,1)} %param.18) | copy-start | bytes 6291460
  7.2 115.6 %all-gather.3.cloned.1.call-start = ((), (), s32[]{:S(2)}) async-start(), calls=%async_computation.5 | async-start | bytes 2228224 | tf_op jit(solution)/shard_map/all_gather | solution.py:77
  9.0 113.8 %all-gather.5.cloned.1.call-start = ((), (), s32[]{:S(2)}) async-start(), calls=%async_computation.6 | async-start | bytes 2228224 | tf_op jit(solution)/shard_map/all_gather | solution.py:76
  81.4 8.8 %copy-start.21 = (bf16[64,32]{0,1:T(8,128)(2,1)S(1)}, bf16[64,32]{0,1:T(8,128)(2,1)}, u32[]{:S(2)}) copy-start(bf16[64,32]{0,1:T(8,128)(2,1)} %param.26) | copy-start | bytes 12292
  81.4 8.9 %copy-start.22 = (bf16[64,32]{0,1:T(8,128)(2,1)S(1)}, bf16[64,32]{0,1:T(8,128)(2,1)}, u32[]{:S(2)}) copy-start(bf16[64,32]{0,1:T(8,128)(2,1)} %param.25) | copy-start | bytes 12292
  85.7 19.2 %all-to-all-start.2 = ((bf16[8,2,32768]{2,1,0:T(2,128)(2,1)}), bf16[8,2,32768]{2,1,0:T(2,128)(2,1)}, u32[]{:S(2)}, u32[]{:S(2)}) async-start(bf16[8,2,32768]{2,1,0:T(2,128)(2,1)} %reshape.90), calls=%async_computation.2 | async-start | bytes 2097152 | tf_op jit(solution)/shard_map/all_to_all | solution.py:20
  90.0 190.2 %reduce-scatter.2.cloned.1.call-start = ((), (), s32[]{:S(2)}) async-start(), calls=%async_computation.7 | async-start | bytes 4718592 | tf_op jit(solution)/shard_map/reduce_scatter | solution.py:116
  132.2 3.1 copy-start.1
  132.2 3.5 %copy-start.27 = (bf16[256,32,128]{2,0,1:T(8,128)(2,1)S(1)}, bf16[256,32,128]{2,0,1:T(8,128)(2,1)}, u32[]{:S(2)}) copy-start(bf16[256,32,128]{2,0,1:T(8,128)(2,1)} %get-tuple-element.192) | copy-start | bytes 6291460 | tf_op jit(solution)/shard_map/while
  144.3 3.1 copy-start.1
  144.3 3.5 %copy-start.27 = (bf16[256,32,128]{2,0,1:T(8,128)(2,1)S(1)}, bf16[256,32,128]{2,0,1:T(8,128)(2,1)}, u32[]{:S(2)}) copy-start(bf16[256,32,128]{2,0,1:T(8,128)(2,1)} %get-tuple-element.192) | copy-start | bytes 6291460 | tf_op jit(solution)/shard_map/while
  156.4 3.1 copy-start.1
  156.4 3.5 %copy-start.27 = (bf16[256,32,128]{2,0,1:T(8,128)(2,1)S(1)}, bf16[256,32,128]{2,0,1:T(8,128)(2,1)}, u32[]{:S(2)}) copy-start(bf16[256,32,128]{2,0,1:T(8,128)(2,1)} %get-tuple-element.192) | copy-start | bytes 6291460 | tf_op jit(solution)/shard_map/while
  168.6 3.1 copy-start.1
  168.6 3.5 %copy-start.27 = (bf16[256,32,128]{2,0,1:T(8,128)(2,1)S(1)}, bf16[256,32,128]{2,0,1:T(8,128)(2,1)}, u32[]{:S(2)}) copy-start(bf16[256,32,128]{2,0,1:T(8,128)(2,1)} %get-tuple-element.192) | copy-start | bytes 6291460 | tf_op jit(solution)/shard_map/while
  180.7 3.1 copy-start.1
  180.7 3.5 %copy-start.27 = (bf16[256,32,128]{2,0,1:T(8,128)(2,1)S(1)}, bf16[256,32,128]{2,0,1:T(8,128)(2,1)}, u32[]{:S(2)}) copy-start(bf16[256,32,128]{2,0,1:T(8,128)(2,1)} %get-tuple-element.192) | copy-start | bytes 6291460 | tf_op jit(solution)/shard_map/while
  192.8 3.5 %copy-start.27 = (bf16[256,32,128]{2,0,1:T(8,128)(2,1)S(1)}, bf16[256,32,128]{2,0,1:T(8,128)(2,1)}, u32[]{:S(2)}) copy-start(bf16[256,32,128]{2,0,1:T(8,128)(2,1)} %get-tuple-element.192) | copy-start | bytes 6291460 | tf_op jit(solution)/shard_map/while
  204.9 3.5 %copy-start.27 = (bf16[256,32,128]{2,0,1:T(8,128)(2,1)S(1)}, bf16[256,32,128]{2,0,1:T(8,128)(2,1)}, u32[]{:S(2)}) copy-start(bf16[256,32,128]{2,0,1:T(8,128)(2,1)} %get-tuple-element.192) | copy-start | bytes 6291460 | tf_op jit(solution)/shard_map/while
  217.0 3.1 copy-start.1
  217.0 3.5 %copy-start.27 = (bf16[256,32,128]{2,0,1:T(8,128)(2,1)S(1)}, bf16[256,32,128]{2,0,1:T(8,128)(2,1)}, u32[]{:S(2)}) copy-start(bf16[256,32,128]{2,0,1:T(8,128)(2,1)} %get-tuple-element.192) | copy-start | bytes 6291460 | tf_op jit(solution)/shard_map/while
  284.2 18.1 %all-to-all-start.3 = ((bf16[128,2,512]{2,1,0:T(2,128)(2,1)}), bf16[128,2,512]{2,1,0:T(2,128)(2,1)}, u32[]{:S(2)}, u32[]{:S(2)}) async-start(bf16[128,2,512]{2,1,0:T(2,128)(2,1)} %reshape.92), calls=%async_computation.4 | async-start | bytes 524288 | tf_op jit(solution)/shard_map/all_to_all | solution.py:117
  291.8 15.3 %copy-start.23 = (f32[64]{0:T(128)S(1)}, f32[64]{0:T(128)}, u32[]{:S(2)}) copy-start(f32[64]{0:T(128)} %param.27) | copy-start | bytes 772
  291.8 15.4 %copy-start.11 = (f32[2,1024]{1,0:T(2,128)}, f32[2,1024]{1,0:T(2,128)S(1)}, u32[]{:S(2)}) copy-start(f32[2,1024]{1,0:T(2,128)S(1)} %add_rsqrt_fusion) | copy-start | bytes 24580
  (24 other events, 38.2 us)
Sparse Core Ops, SparseCore 0:
  10.8 58.4 all-gather.2
  71.6 48.3 all-gather.4
  228.8 51.2 reduce-scatter.1
where the time goes:
time: 325 us; the launch traced here: 323 us
  local copies, waits for them, and re-layouts  78.6 us (24%)
  matrix products  75.6 us (23%)
  waiting for transfers between devices  72.8 us (22%)
  blocking collectives  53.2 us (16%)
  other arithmetic  16.4 us (5%)
  between operations  14.2 us (4%)
  starting transfers between devices  12 us (4%)
    reduce_scatter x1, waiting for transfers between devices, per_device(): lax.psum_scatter(partial_terms, 'col', scatter_dimension=2, tiled=True)  47.7 us
    convert_element_type x8, local copies, waits for them, and re-layouts, single_tile(): tensor_product_derivative = jnp.einsum('ijp,kp->ijk', grad_rows, outer_pa...  31.2 us
    all_to_all x1, blocking collectives, per_device(): lax.all_to_all(regroup(logits), ('row', 'col'), split_axis=2, concat_axis...  30.8 us
    unnamed x64, local copies, waits for them, and re-layouts  26.4 us
    dot_general x8, matrix products, single_tile(): jnp.einsum('ijce,scj->sei', tensor_product_derivative, left_all, preferre...  24.8 us
    dot_general x8, matrix products, single_tile(): jnp.einsum('ijp,kp->ijk', grad_rows, outer_pair_weight, preferred_element...  24.2 us
    all_to_all x1, blocking collectives, regroup(): lax.all_to_all(logit_tile, 'col', split_axis=1, concat_axis=2, tiled=True)  22.4 us
    all_to_all x1, waiting for transfers between devices, regroup(): lax.all_to_all(logit_tile, 'col', split_axis=1, concat_axis=2, tiled=True)  14.5 us
  transfers between devices with their start and end apart: 5, of which 3 were waited for; matrix products, arithmetic and copies ran while one was open for 13% of the time, Pallas kernels for 0%

commit v1 on v0

v1 whole, which is shorter than its diff:
```python
import functools

import jax
import jax.numpy as jnp
from jax import lax
from jax.experimental import pallas as pl
from jax.experimental.pallas import tpu as pltpu
from jax.sharding import PartitionSpec as P

MESH = pl.DeviceIdType.MESH
BF = jnp.bfloat16
F32 = jnp.float32
VM = pl.BlockSpec(memory_space=pltpu.VMEM)


def dot_nt(a, b):
    return lax.dot_general(a, b, (((1,), (1,)), ((), ())), preferred_element_type=F32)


def dot_nn(a, b):
    return lax.dot_general(a, b, (((1,), (0,)), ((), ())), preferred_element_type=F32)


def place():
    row, col = lax.axis_index("row"), lax.axis_index("col")
    return row, col, row // 8, (row // 2) % 4, row % 2, col // 4, col % 4


def full_barrier(row, col):
    barrier = pltpu.get_barrier_semaphore()
    me = row * 8 + col

    def greet(step, _):
        other = (me + step) % 128
        pl.semaphore_signal(
            barrier, inc=1, device_id={"row": other // 8, "col": other % 8}, device_id_type=MESH
        )
        return 0

    lax.fori_loop(1, 128, greet, 0)
    pl.semaphore_wait(barrier, 127)


def remote(src, dst, send, recv, row, col):
    return pltpu.make_async_remote_copy(
        src, dst, send, recv, device_id={"row": row, "col": col}, device_id_type=MESH
    )


def pair_index(pos):
    block, m = pos // 4, pos % 4
    return 2 * block + m % 2 + 16 * (m // 2)


def bias_columns(bias_ref):
    return jnp.broadcast_to(bias_ref[...], (128, 64)).T


def front_kernel(
    a_ref, tgt_ref, wd_ref, bias_ref, lhs_ref, rhs_ref, lg_ref, lrg_ref,
    a32, t_buf, b_buf, ra_buf, rb_buf, s32, loc_sem, m_send, m_recv, ra_send, ra_recv, rb_send, rb_recv,
    g_send, g_recv, p_send, p_recv,
):
    row, col, yh, x, k, yl, z = place()
    chip = row // 2
    full_barrier(row, col)
    mine = pl.ds(pl.multiple_of(row * 16, 16), 16)
    for side, ref in ((0, lhs_ref), (1, rhs_ref)):
        for s in range(16):
            s32[pl.ds(s * 32, 32), :] = ref[s].astype(F32)
        for e in range(32):
            lrg_ref[side, mine, e * 128 : (e + 1) * 128] = s32[pl.ds(e, 16, stride=32), :].astype(BF)
    wdt = wd_ref[...].astype(F32).T.astype(BF)
    bias = bias_columns(bias_ref)

    @pl.loop(0, 64)
    def _(i):
        a32[pl.ds(pl.multiple_of(i * 128, 128), 128), :] = a_ref[i].astype(F32)

    diag = x == z
    same_y = yh == yl
    sends = []
    for q in range(4):
        for kk in range(2):

            @pl.loop(0, 8)
            def _(p):
                ii = pair_index(q * 8 + p) + 64 * kk
                first = a32[pl.ds(ii + 32 * k, 64, stride=128), :]
                second = a32[pl.ds(ii + 32 * (1 - k), 64, stride=128), :]
                both = jnp.concatenate([first, second], axis=0).astype(BF)
                t_buf[kk, q, p] = (dot_nt(wdt, both) + bias).astype(BF)

            src = t_buf.at[kk, q]
            final = remote(src, b_buf.at[k, q], m_send.at[kk, q], m_recv.at[k, q], 2 * col + kk, chip)
            local = pltpu.make_async_copy(src, b_buf.at[k, q], loc_sem.at[q])
            home = jnp.logical_and(diag, same_y)
            own = jnp.logical_and(home, k == kk)
            if q % 2 == 0:
                direct = jnp.logical_and(jnp.logical_or(diag, same_y), jnp.logical_not(own))
                hop = remote(
                    src, ra_buf.at[kk, q // 2], m_send.at[kk, q], ra_recv.at[kk, q // 2],
                    yl * 8 + x * 2 + k, yh * 4 + z,
                )
            else:
                direct = jnp.logical_and(diag, jnp.logical_not(own))
                slot = (z - x + 3) % 4
                hop = remote(
                    src, rb_buf.at[slot, kk, q // 2], m_send.at[kk, q], rb_recv.at[slot, kk, q // 2],
                    yl * 8 + x * 2 + k, yh * 4 + x,
                )
            relayed = jnp.logical_not(jnp.logical_or(direct, own))
            pl.when(own)(local.start)
            pl.when(direct)(final.start)
            pl.when(relayed)(hop.start)
            sends.append((own, local, final))
    partner = row + 1 - 2 * k
    g_copies = []
    for step in range(1, 8):
        there = (row + 2 * step) % 16
        cp = remote(
            lrg_ref.at[:, mine], lrg_ref.at[:, mine], g_send.at[step], g_recv.at[step], there, col
        )
        cp.start()
        g_copies.append(cp)
    cp = remote(lrg_ref.at[:, mine], lrg_ref.at[:, mine], p_send.at[0], p_recv.at[0], partner, col)
    cp.start()
    p_copies = [cp]
    relay_a = jnp.logical_not(jnp.logical_or(diag, same_y))
    fa, fb = [], []
    for j in range(2):
        for kk in range(2):
            cp = remote(
                ra_buf.at[kk, j], b_buf.at[k, 2 * j], ra_send.at[kk, j], m_recv.at[k, 2 * j],
                2 * (yh * 4 + z) + kk, yl * 4 + x,
            )

            @pl.when(relay_a)
            def _():
                remote(
                    ra_buf.at[kk, j], ra_buf.at[kk, j], ra_send.at[kk, j], ra_recv.at[kk, j], row, col
                ).wait_recv()
                cp.start()

            fa.append(cp)
            for slot in range(3):
                zs = (x + 1 + slot) % 4
                cp2 = remote(
                    rb_buf.at[slot, kk, j], b_buf.at[k, 2 * j + 1], rb_send.at[slot, kk, j],
                    m_recv.at[k, 2 * j + 1], 2 * (yh * 4 + zs) + kk, yl * 4 + x,
                )

                @pl.when(diag)
                def _():
                    remote(
                        rb_buf.at[slot, kk, j], rb_buf.at[slot, kk, j], rb_send.at[slot, kk, j],
                        rb_recv.at[slot, kk, j], row, col,
                    ).wait_recv()
                    cp2.start()

                fb.append(cp2)
    lane = lax.broadcasted_iota(jnp.int32, (64, 128), 1)
    level = lax.broadcasted_iota(jnp.int32, (64, 128), 0)
    low = lane < 64
    home = jnp.logical_and(diag, same_y)
    for q in range(4):
        for kk in range(2):
            own = jnp.logical_and(home, k == kk)

            @pl.when(jnp.logical_not(own))
            def _():
                remote(
                    t_buf.at[0, q], b_buf.at[kk, q], m_send.at[0, q], m_recv.at[kk, q], row, col
                ).wait_recv()

            @pl.when(own)
            def _():
                pltpu.make_async_copy(t_buf.at[kk, q], b_buf.at[kk, q], loc_sem.at[q]).wait()

        @pl.loop(0, 8)
        def _(p):
            pos = q * 8 + p
            ii = pair_index(pos)
            b0 = b_buf[0, q, p].astype(F32)
            b1 = b_buf[1, q, p].astype(F32)
            mirrored = (
                jnp.where(low, b0, b1),
                pltpu.roll(jnp.where(low, b1, b0), 64, 1),
            )
            for h in range(2):
                i = ii + 32 * h
                own_logits = (dot_nt(wdt, a_ref[i]) + bias).astype(BF).astype(F32)
                sym = own_logits + mirrored[h]
                top = jnp.max(sym, axis=0, keepdims=True)
                ex = jnp.exp(sym - top)
                prob = ex / jnp.sum(ex, axis=0, keepdims=True)
                tgt = tgt_ref[pl.ds(i, 1), :]
                hot = jnp.where(level == tgt, 1.0, 0.0)
                lg_ref[pos, h] = (2.0 * (prob - hot)).astype(BF)

    for step in range(1, 8):
        source = (row - 2 * step + 16) % 16
        rows = pl.ds(pl.multiple_of(source * 16, 16), 16)
        remote(
            lrg_ref.at[:, rows], lrg_ref.at[:, rows], g_send.at[step], g_recv.at[step], row, col
        ).wait_recv()
        cp = remote(
            lrg_ref.at[:, rows], lrg_ref.at[:, rows], p_send.at[step], p_recv.at[step], partner, col
        )
        cp.start()
        p_copies.append(cp)
    for step in range(8):
        source = (partner - 2 * step + 16) % 16
        rows = pl.ds(pl.multiple_of(source * 16, 16), 16)
        remote(
            lrg_ref.at[:, rows], lrg_ref.at[:, rows], p_send.at[step], p_recv.at[step], row, col
        ).wait_recv()
    for cp in g_copies + p_copies:
        cp.wait_send()
    for own, local, final in sends:
        pl.when(jnp.logical_not(own))(final.wait_send)
    for cp in fa:
        pl.when(relay_a)(cp.wait_send)
    for cp in fb:
        pl.when(diag)(cp.wait_send)


def front(a, tgt, wd, bias, lhs, rhs):
    dma = pltpu.SemaphoreType.DMA
    return pl.pallas_call(
        front_kernel,
        out_shape=(
            jax.ShapeDtypeStruct((32, 2, 64, 128), BF),
            jax.ShapeDtypeStruct((2, 256, 4096), BF),
        ),
        in_specs=[VM] * 6,
        out_specs=(VM, VM),
        scratch_shapes=[
            pltpu.VMEM((8192, 128), F32),
            pltpu.VMEM((2, 4, 8, 64, 128), BF),
            pltpu.VMEM((2, 4, 8, 64, 128), BF),
            pltpu.VMEM((2, 2, 8, 64, 128), BF),
            pltpu.VMEM((3, 2, 2, 8, 64, 128), BF),
            pltpu.VMEM((512, 128), F32),
            dma((4,)),
            dma((2, 4)),
            dma((2, 4)),
            dma((2, 2)),
            dma((2, 2)),
            dma((3, 2, 2)),
            dma((3, 2, 2)),
            dma((8,)),
            dma((8,)),
            dma((8,)),
            dma((8,)),
        ],
        compiler_params=pltpu.CompilerParams(
            collective_id=0, has_side_effects=True, vmem_limit_bytes=60 << 20
        ),
        name="front",
    )(a, tgt, wd, bias, lhs, rhs)


def middle_kernel(lg_ref, lrg_ref, wd_ref, wo_ref, g_ref, part_ref, w32, wec, xs, o32):
    wd = wd_ref[...]
    wdt = wd.astype(F32).T.astype(BF)
    w32[...] = wo_ref[...].astype(F32)
    for e in range(32):
        wec[pl.ds(e * 32, 32), :] = w32[pl.ds(e, 32, stride=32), :].astype(BF)

    @pl.loop(0, 8)
    def _(block):
        @pl.loop(0, 4)
        def _(m):
            pos = block * 4 + m
            ii = pair_index(pos)
            pair = jnp.concatenate([lg_ref[pos, 0], lg_ref[pos, 1]], axis=1)
            gt = dot_nn(wd, pair).astype(BF)
            for h in range(2):
                lgt = lg_ref[pos, h].astype(F32).T.astype(BF)
                g_ref[ii + 32 * h] = dot_nn(lgt, wdt).astype(BF)
            for side, w in ((0, wec), (1, wo_ref)):
                for n in range(4):
                    u = dot_nn(w[pl.ds(n * 256, 256), :], gt).astype(BF)
                    for h in range(2):
                        base = pl.multiple_of((m % 2) * 128 + (m // 2) * 32 + 64 * h, 32)
                        for f in range(8):
                            e = n * 8 + f
                            xs[side, pl.ds(base, 32), e * 128 : (e + 1) * 128] = u[
                                f * 32 : (f + 1) * 32, h * 128 : (h + 1) * 128
                            ]

        for side in range(2):
            out = dot_nt(lrg_ref[1 - side], xs[side])
            for half in range(2):
                o32[...] = out[:, half * 128 : (half + 1) * 128]
                for w in range(16):
                    part_ref[w // 2, block, side, half, (w % 2) * 16 : (w % 2) * 16 + 16, :] = o32[
                        pl.ds(w, 16, stride=16), :
                    ].astype(BF)


def middle(lg, lrg, wd, wo):
    return pl.pallas_call(
        middle_kernel,
        out_shape=(
            jax.ShapeDtypeStruct((64, 128, 128), BF),
            jax.ShapeDtypeStruct((8, 8, 2, 2, 32, 128), BF),
        ),
        in_specs=[VM] * 4,
        out_specs=(VM, VM),
        scratch_shapes=[
            pltpu.VMEM((1024, 128), F32),
            pltpu.VMEM((1024, 128), BF),
            pltpu.VMEM((2, 256, 4096), BF),
            pltpu.VMEM((256, 128), F32),
        ],
        compiler_params=pltpu.CompilerParams(vmem_limit_bytes=60 << 20),
        name="middle",
    )(lg, lrg, wd, wo)


def reduce_kernel(part_ref, fin_ref, got, s32, s16, r_send, r_recv, a_send, a_recv):
    row, col, yh, x, k, yl, z = place()
    full_barrier(row, col)
    copies = []
    for step in range(1, 8):
        there = (col + step) % 8
        cp = remote(
            part_ref.at[there], got.at[step - 1], r_send.at[step - 1], r_recv.at[step - 1], row, there
        )
        cp.start()
        copies.append(cp)
    for cp in copies:
        cp.wait_recv()

    @pl.loop(0, 8)
    def _(block):
        for side in range(2):
            for half in range(2):
                total = part_ref[col, block, side, half].astype(F32)
                for step in range(7):
                    total += got[step, block, side, half].astype(F32)
                q = side * 16 + block * 2 + half
                for t in range(2):
                    s32[pl.ds(t * 32 + q, 16, stride=64), :] = total[t * 16 : (t + 1) * 16]

    for there in range(16):
        s16[there] = s32[pl.ds(there * 64, 64), :].astype(BF)
    fin_ref[row] = s16[row]
    for step in range(1, 16):
        there = (row + step) % 16
        cp = remote(s16.at[there], fin_ref.at[row], a_send.at[step], a_recv.at[step], there, col)
        cp.start()
        copies.append(cp)
    for step in range(1, 16):
        source = (row - step + 16) % 16
        remote(
            s16.at[0], fin_ref.at[source], a_send.at[step], a_recv.at[step], row, col
        ).wait_recv()
    for cp in copies:
        cp.wait_send()


def reduce(part):
    dma = pltpu.SemaphoreType.DMA
    return pl.pallas_call(
        reduce_kernel,
        out_shape=jax.ShapeDtypeStruct((16, 64, 128), BF),
        in_specs=[VM],
        out_specs=VM,
        scratch_shapes=[
            pltpu.VMEM((7, 8, 2, 2, 32, 128), BF),
            pltpu.VMEM((1024, 128), F32),
            pltpu.VMEM((16, 64, 128), BF),
            dma((7,)),
            dma((7,)),
            dma((16,)),
            dma((16,)),
        ],
        compiler_params=pltpu.CompilerParams(
            collective_id=1, has_side_effects=True, vmem_limit_bytes=60 << 20
        ),
        name="reduce",
    )(part)


def norm_forward(v):
    centered = v - jnp.mean(v, axis=0, keepdims=True)
    inv = lax.rsqrt(jnp.mean(centered * centered, axis=0, keepdims=True) + 1e-05)
    return centered * inv, inv


def norm_backward(g, normed, inv):
    first = jnp.mean(g, axis=0, keepdims=True)
    second = jnp.mean(g * normed, axis=0, keepdims=True)
    return inv * (g - first - normed * second)


def column(ref):
    return jnp.broadcast_to(ref[...], (128, ref.shape[1])).T[:, :1]


def tail_kernel(
    fin_ref, side_ref, arrive_ref, lw_ref, rw_ref, og_ref, tg_ref, gw_ref, uw_ref, dw_ref, out_ref, wts
):
    lanes = 256
    gwt = gw_ref[...].astype(F32).T.astype(BF)
    uwt = uw_ref[...].astype(F32).T.astype(BF)
    dwt = dw_ref[...].astype(F32).T.astype(BF)
    gw, uw, dw = gw_ref[...], uw_ref[...], dw_ref[...]
    lw, rw = lw_ref[...], rw_ref[...]
    ab = jnp.concatenate([lw] * 4 + [rw] * 4, axis=1)
    og, tg = column(og_ref), column(tg_ref)
    group = lax.broadcasted_iota(jnp.int32, (16, 128), 1) // 32
    zero = jnp.zeros((16, 128), BF)

    @pl.loop(0, 2)
    def _(s):
        @pl.loop(0, 1024 // lanes)
        def _(n):
            for r in range(lanes // 64):
                for side in range(2):
                    rows = fin_ref[n * (lanes // 64) + r, pl.ds(pl.multiple_of(s * 32 + side * 16, 16), 16), :]
                    for lo in range(4):
                        wts[pl.ds(r * 64 + lo * 16, 16), side * 128 : side * 128 + 128] = jnp.where(
                            group == lo, rows, zero
                        )
            at = pl.ds(pl.multiple_of(n * lanes, lanes), lanes)
            ng = (dot_nt(ab, wts[...]) * (1.0 / 256)).astype(BF).astype(F32)
            v = side_ref[s, :, at].astype(F32)
            n1, inv1 = norm_forward(v)
            nin = (n1 * tg).astype(BF)
            gate = dot_nn(gwt, nin)
            up = dot_nn(uwt, nin)
            sig = jax.nn.sigmoid(gate)
            act = gate * sig
            hidden = (act * up).astype(BF)
            n2, inv2 = norm_forward(v + dot_nn(dwt, hidden))
            mid = arrive_ref[s, :, at].astype(F32) + norm_backward(ng * og, n2, inv2)
            hg = dot_nn(dw, mid.astype(BF))
            gg = (hg * up * sig * (1.0 + gate * (1.0 - sig))).astype(BF)
            ug = (hg * act).astype(BF)
            nrg = dot_nn(gw, gg) + dot_nn(uw, ug)
            out_ref[s, :, at] = (mid + norm_backward(nrg * tg, n1, inv1)).astype(BF)


def tail(fin, side, arrive, lw, rw, og, tg, gw, uw, dw):
    return pl.pallas_call(
        tail_kernel,
        out_shape=jax.ShapeDtypeStruct((2, 64, 1024), BF),
        in_specs=[VM] * 10,
        out_specs=VM,
        scratch_shapes=[pltpu.VMEM((256, 256), BF)],
        compiler_params=pltpu.CompilerParams(vmem_limit_bytes=40 << 20),
        name="tail",
    )(fin, side, arrive, lw, rw, og, tg, gw, uw, dw)


def per_device(
    pair_activation, target_distance_bins, distogram_weight, distogram_bias, outer_pair_weight,
    stored_lhs_operand, stored_rhs_operand, left_projection_weight, right_projection_weight,
    outer_mean_norm_gain, transition_norm_gain, gate_weight, up_weight, down_weight,
    side_stack_entry, arriving_stack_derivative,
):
    lg, lrg = front(
        pair_activation, target_distance_bins, distogram_weight, distogram_bias.reshape(1, -1),
        stored_lhs_operand, stored_rhs_operand,
    )
    g, part = middle(lg, lrg, distogram_weight, outer_pair_weight)
    fin = reduce(part)
    out = tail(
        fin, side_stack_entry, arriving_stack_derivative, left_projection_weight,
        right_projection_weight, outer_mean_norm_gain.reshape(1, -1),
        transition_norm_gain.reshape(1, -1), gate_weight, up_weight, down_weight,
    )
    return g, out


def solution(mesh):
    return jax.shard_map(
        per_device,
        mesh=mesh,
        in_specs=(
            P("row", "col", None),
            P("row", "col"),
            P(),
            P(),
            P(),
            P("row", None, "col"),
            P("row", None, "col"),
            P(),
            P(),
            P(),
            P(),
            P(),
            P(),
            P(),
            P(("row", "col"), None, None),
            P(("row", "col"), None, None),
        ),
        out_specs=(P("row", "col", None), P(("row", "col"), None, None)),
        check_vma=False,
    )
```

time: 325 us -> 186 us (0.57)
  the two profiles are of different devices: /device:TPU:1 before, /device:TPU:97 now
where the time goes in v1:
time: 186 us; the launch traced here: 185 us
  Pallas kernels  182 us (98%)
  local copies, waits for them, and re-layouts  2.73 us (1%)
    pallas_call x1, Pallas kernels, reduce(): pl.pallas_call(reduce_kernel, out_shape=jax.ShapeDtypeStruct((16, 64, 128...  69.3 us
    pallas_call x1, Pallas kernels, front(): pl.pallas_call(front_kernel, out_shape=(jax.ShapeDtypeStruct((32, 2, 64,...  67.4 us
    pallas_call x1, Pallas kernels, middle(): pl.pallas_call(middle_kernel, out_shape=(jax.ShapeDtypeStruct((64, 128, 1...  36.8 us
    pallas_call x1, Pallas kernels, tail(): pl.pallas_call(tail_kernel, out_shape=jax.ShapeDtypeStruct((2, 64, 1024),...  8.27 us

profile of v1, /device:TPU:97, one launch (start us, length us, event | category | flops | bytes accessed | tf_op | source)
XLA Modules:
  0.0 185.3 jit_solution(12199288261455576772)
XLA Ops:
  0.6 1.4 copy.18.wd_ref
  2.1 67.4 %front.1 = (bf16[32,2,64,128]{3,2,1,0:T(8,128)(2,1)}, bf16[2,256,4096]{2,1,0:T(8,128)(2,1)}) custom-call(bf16[64,128,128]{2,1,0:T(8,128)(2,1)} %a_ref.1, s32[64,128]{1,0:T(8,128)} %tgt_ref.1, bf16[128,64]{1,0:T(8,128)(2,1)} %copy.18.wd_ref, f32[1,64]{1,0:T(1,128)} %bitcast.5, bf16[16,32,128]{2,1,0:T(8,128)(2,1)} %lhs_ref.1, bf16[16,32,128]{2,1,0:T(8,128)(2,1)} %rhs_ref.1), custom_call_target="tpu_custom_call" | custom-call | tf_op jit(solution)/shard_map/front/pallas_call | solution.py:230
  69.5 36.8 %middle.1 = (bf16[64,128,128]{2,1,0:T(8,128)(2,1)}, bf16[8,8,2,2,32,128]{5,4,3,2,1,0:T(8,128)(2,1)}) custom-call(bf16[32,2,64,128]{3,2,1,0:T(8,128)(2,1)} %get-tuple-element.6.lg_ref, bf16[2,256,4096]{2,1,0:T(8,128)(2,1)} %get-tuple-element.7.lrg_ref, bf16[128,64]{1,0:T(8,128)(2,1)} %copy.18.wd_ref, bf16[1024,128]{1,0:T(8,128)(2,1)} %wo_ref.1), custom_call_target="tpu_custom_call" | custom-call | tf_op jit(solution)/shard_map/middle/pallas_call | solution.py:304
  106.3 0.0 copy-start.1
  106.3 0.0 copy-start.2
  106.4 0.0 copy-start.3
  106.4 0.0 copy-start.4
  106.4 0.0 copy-start.5
  106.4 0.0 copy-start.6
  106.4 69.3 %reduce.1.fin_ref = bf16[16,64,128]{2,1,0:T(8,128)(2,1)} custom-call(bf16[8,8,2,2,32,128]{5,4,3,2,1,0:T(8,128)(2,1)} %get-tuple-element.9.part_ref), custom_call_target="tpu_custom_call" | custom-call | tf_op jit(solution)/shard_map/reduce/pallas_call | solution.py:367
  175.7 0.0 copy-done.7
  175.7 0.1 copy.22.dw_ref
  175.8 0.0 copy-done.8
  175.8 0.1 copy.20.lw_ref
  175.9 0.0 copy-done.9
  176.0 0.1 copy.21.rw_ref
  176.1 0.0 copy-done.2
  176.1 0.0 copy-done.3
  176.1 0.0 copy-done.4
  176.1 0.0 copy-done.5
  176.1 0.0 copy-done.6
  176.1 0.0 copy-start
  176.1 0.9 copy-done
  177.1 8.3 %tail.1 = bf16[2,64,1024]{2,1,0:T(8,128)(2,1)} custom-call(bf16[16,64,128]{2,1,0:T(8,128)(2,1)S(1)} %copy-done, bf16[2,64,1024]{2,1,0:T(8,128)(2,1)S(1)} %copy-done.1, bf16[2,64,1024]{2,1,0:T(8,128)(2,1)S(1)} %copy-done.2, bf16[64,32]{1,0:T(8,128)(2,1)S(1)} %copy.20.lw_ref, bf16[64,32]{1,0:T(8,128)(2,1)S(1)} %copy.21.rw_ref, f32[1,64]{1,0:T(1,128)S(1)} %bitcast.3, ...), custom_call_target="tpu_custom_call" | custom-call | tf_op jit(solution)/shard_map/tail/pallas_call | solution.py:449
  (4 shorter events, 0.0 us)
Async XLA Ops:
  106.3 69.4 %copy-start.7 = (bf16[256,64]{0,1:T(8,128)(2,1)S(1)}, bf16[256,64]{0,1:T(8,128)(2,1)}, u32[]{:S(2)}) copy-start(bf16[256,64]{0,1:T(8,128)(2,1)} %param.29) | copy-start | bytes 98308
  106.3 69.5 %copy-start.8 = (bf16[64,32]{0,1:T(8,128)(2,1)S(1)}, bf16[64,32]{0,1:T(8,128)(2,1)}, u32[]{:S(2)}) copy-start(bf16[64,32]{0,1:T(8,128)(2,1)} %param.23) | copy-start | bytes 12292
  106.3 69.6 %copy-start.9 = (bf16[64,32]{0,1:T(8,128)(2,1)S(1)}, bf16[64,32]{0,1:T(8,128)(2,1)}, u32[]{:S(2)}) copy-start(bf16[64,32]{0,1:T(8,128)(2,1)} %param.24) | copy-start | bytes 12292
  106.3 69.7 %copy-start.1 = (bf16[2,64,1024]{2,1,0:T(8,128)(2,1)S(1)}, bf16[2,64,1024]{2,1,0:T(8,128)(2,1)}, u32[]{:S(2)}) copy-start(bf16[2,64,1024]{2,1,0:T(8,128)(2,1)} %side_ref.1) | copy-start | bytes 786436
  106.3 69.7 %copy-start.2 = (bf16[2,64,1024]{2,1,0:T(8,128)(2,1)S(1)}, bf16[2,64,1024]{2,1,0:T(8,128)(2,1)}, u32[]{:S(2)}) copy-start(bf16[2,64,1024]{2,1,0:T(8,128)(2,1)} %arrive_ref.1) | copy-start | bytes 786436
  106.4 69.7 %copy-start.3 = (bf16[64,256]{1,0:T(8,128)(2,1)S(1)}, bf16[64,256]{1,0:T(8,128)(2,1)}, u32[]{:S(2)}) copy-start(bf16[64,256]{1,0:T(8,128)(2,1)} %gw_ref.1) | copy-start | bytes 98308
  106.4 69.7 %copy-start.4 = (bf16[64,256]{1,0:T(8,128)(2,1)S(1)}, bf16[64,256]{1,0:T(8,128)(2,1)}, u32[]{:S(2)}) copy-start(bf16[64,256]{1,0:T(8,128)(2,1)} %uw_ref.1) | copy-start | bytes 98308
  106.4 69.7 %copy-start.5 = (f32[64]{0:T(128)S(1)}, f32[64]{0:T(128)}, u32[]{:S(2)}) copy-start(f32[64]{0:T(128)} %param.25) | copy-start | bytes 772
  106.4 69.7 %copy-start.6 = (f32[64]{0:T(128)S(1)}, f32[64]{0:T(128)}, u32[]{:S(2)}) copy-start(f32[64]{0:T(128)} %param.26) | copy-start | bytes 772
  176.1 1.0 copy-start

commit v2 on v1

v2 whole, which is shorter than its diff:
```python
import functools

import jax
import jax.numpy as jnp
from jax import lax
from jax.experimental import pallas as pl
from jax.experimental.pallas import tpu as pltpu
from jax.sharding import PartitionSpec as P

MESH = pl.DeviceIdType.MESH
BF = jnp.bfloat16
F32 = jnp.float32
VM = pl.BlockSpec(memory_space=pltpu.VMEM)


def dot_nt(a, b):
    return lax.dot_general(a, b, (((1,), (1,)), ((), ())), preferred_element_type=F32)


def dot_nn(a, b):
    return lax.dot_general(a, b, (((1,), (0,)), ((), ())), preferred_element_type=F32)


def place():
    row, col = lax.axis_index("row"), lax.axis_index("col")
    return row, col, row // 8, (row // 2) % 4, row % 2, col // 4, col % 4


def full_barrier(row, col):
    barrier = pltpu.get_barrier_semaphore()
    me = row * 8 + col

    def greet(step, _):
        other = (me + step) % 128
        pl.semaphore_signal(
            barrier, inc=1, device_id={"row": other // 8, "col": other % 8}, device_id_type=MESH
        )
        return 0

    lax.fori_loop(1, 128, greet, 0)
    pl.semaphore_wait(barrier, 127)


def remote(src, dst, send, recv, row, col):
    return pltpu.make_async_remote_copy(
        src, dst, send, recv, device_id={"row": row, "col": col}, device_id_type=MESH
    )


def pair_index(pos):
    block, m = pos // 4, pos % 4
    return 2 * block + m % 2 + 16 * (m // 2)


def bias_columns(bias_ref):
    return jnp.broadcast_to(bias_ref[...], (128, 64)).T


def arrived(dst, recv, row, col):
    remote(dst, dst, recv, recv, row, col).wait_recv()


BLOCK_Y = (True, False, True, False, True, False, True, True)


def main_kernel(
    a_ref, tgt_ref, wd_ref, bias_ref, wo_ref, lhs_ref, rhs_ref, g_hbm, fin_ref,
    a32, t_buf, b_buf, ra_buf, rb_buf, s32, lrg, g_buf, w32, wec, xs, o32, part, got_y, got_z, fin32, fin16, own_buf, gt_buf,
    loc_sem, m_send, m_recv, ra_send, ra_recv, rb_send, rb_recv,
    gx_send, gx_recv, p_send, p_recv, out_sem, y_send, y_recv, z_send, z_recv, f_send, f_recv,
):
    row, col, yh, x, k, yl, z = place()
    chip = row // 2
    diag = x == z
    same_y = yh == yl
    home = jnp.logical_and(diag, same_y)
    partner = row + 1 - 2 * k
    sends = []

    def go(cp, when=None):
        if when is None:
            cp.start()
        else:
            pl.when(when)(cp.start)
        sends.append((cp, when))

    def block_rows(r):
        return pl.ds(pl.multiple_of(r * 16, 16), 16)

    def x_row(r, d):
        return (r // 8) * 8 + (((r // 2) % 4 + d) % 4) * 2 + r % 2

    full_barrier(row, col)
    mine = block_rows(row)
    for side, ref in ((0, lhs_ref), (1, rhs_ref)):
        for s in range(16):
            s32[pl.ds(s * 32, 32), :] = ref[s].astype(F32)
        for e in range(32):
            lrg[side, mine, e * 128 : (e + 1) * 128] = s32[pl.ds(e, 16, stride=32), :].astype(BF)

    def whole(r):
        return lrg.at[:, block_rows(r)]

    def share(r, slot):
        go(remote(whole(r), whole(r), p_send.at[slot], p_recv.at[slot], partner, col))

    def gather_send(r, slot, there, side=None):
        ref = whole(r) if side is None else lrg.at[side, block_rows(r)]
        go(remote(ref, ref, gx_send.at[slot], gx_recv.at[slot], there, col))

    def gather_wait(r, slot, side=None):
        ref = whole(r) if side is None else lrg.at[side, block_rows(r)]
        arrived(ref, gx_recv.at[slot], row, col)

    flip = (row + 8) % 16
    left, right = x_row(row, 3), x_row(row, 1)
    flip_left, flip_right = x_row(flip, 3), x_row(flip, 1)
    far, flip_far = x_row(row, 2), x_row(flip, 2)
    gather_send(row, 0, flip)
    gather_send(row, 1, right)
    gather_send(row, 2, left)
    share(row, 0)

    wdt = wd_ref[...]
    wd = wdt.astype(F32).T.astype(BF)
    bias = bias_columns(bias_ref)

    @pl.loop(0, 64, unroll=4)
    def _(i):
        a32[pl.ds(pl.multiple_of(i * 128, 128), 128), :] = a_ref[i].astype(F32)

    for q in range(4):
        for kk in range(2):

            @pl.loop(0, 8, unroll=8)
            def _(p):
                ii = pair_index(q * 8 + p) + 64 * kk
                first = a32[pl.ds(ii + 32 * k, 64, stride=128), :]
                second = a32[pl.ds(ii + 32 * (1 - k), 64, stride=128), :]
                both = jnp.concatenate([first, second], axis=0).astype(BF)
                t_buf[kk, q, p] = (dot_nt(wdt, both) + bias).astype(BF)

            src = t_buf.at[kk, q]
            final = remote(src, b_buf.at[k, q], m_send.at[kk, q], m_recv.at[k, q], 2 * col + kk, chip)
            local = pltpu.make_async_copy(src, b_buf.at[k, q], loc_sem.at[q])
            own = jnp.logical_and(home, k == kk)
            if q % 2 == 0:
                direct = jnp.logical_and(jnp.logical_or(diag, same_y), jnp.logical_not(own))
                hop = remote(
                    src, ra_buf.at[kk, q // 2], m_send.at[kk, q], ra_recv.at[kk, q // 2],
                    yl * 8 + x * 2 + k, yh * 4 + z,
                )
            else:
                direct = jnp.logical_and(diag, jnp.logical_not(own))
                slot = (z - x + 3) % 4
                hop = remote(
                    src, rb_buf.at[slot, kk, q // 2], m_send.at[kk, q], rb_recv.at[slot, kk, q // 2],
                    yl * 8 + x * 2 + k, yh * 4 + x,
                )
            relayed = jnp.logical_not(jnp.logical_or(direct, own))
            pl.when(own)(local.start)
            pl.when(direct)(final.start)
            pl.when(relayed)(hop.start)
            sends.append((final, jnp.logical_not(own)))

    w32[...] = wo_ref[...].astype(F32)
    for e in range(32):
        wec[pl.ds(e * 32, 32), :] = w32[pl.ds(e, 32, stride=32), :].astype(BF)

    gather_wait(flip, 0)
    gather_send(flip, 3, right)
    gather_send(flip, 4, left)
    share(flip, 1)

    relay_a = jnp.logical_not(jnp.logical_or(diag, same_y))

    def relay(j):
        for kk in range(2):
            pl.when(relay_a)(functools.partial(arrived, ra_buf.at[kk, j], ra_recv.at[kk, j], row, col))
            go(
                remote(
                    ra_buf.at[kk, j], b_buf.at[k, 2 * j], ra_send.at[kk, j], m_recv.at[k, 2 * j],
                    2 * (yh * 4 + z) + kk, yl * 4 + x,
                ),
                relay_a,
            )
        for kk in range(2):
            for slot in range(3):
                zs = (x + 1 + slot) % 4
                pl.when(diag)(
                    functools.partial(arrived, rb_buf.at[slot, kk, j], rb_recv.at[slot, kk, j], row, col)
                )
                go(
                    remote(
                        rb_buf.at[slot, kk, j], b_buf.at[k, 2 * j + 1], rb_send.at[slot, kk, j],
                        m_recv.at[k, 2 * j + 1], 2 * (yh * 4 + zs) + kk, yl * 4 + x,
                    ),
                    diag,
                )

    @pl.loop(0, 64, unroll=8)
    def _(i):
        own_buf[i] = (dot_nt(wdt, a_ref[i]) + bias).astype(BF)

    relay(0)
    relay(1)

    def pass_on(near_left, near_right, slots, shares):
        gather_wait(near_left, slots[0])
        gather_send(near_left, slots[2], right, 0)
        share(near_left, shares[0])
        gather_wait(near_right, slots[1])
        gather_send(near_right, slots[3], left, 1)
        share(near_right, shares[1])

    lane = lax.broadcasted_iota(jnp.int32, (64, 128), 1)
    level = lax.broadcasted_iota(jnp.int32, (64, 128), 0)
    low = lane < 64
    out_copies = []
    for q in range(4):
        for kk in range(2):
            own = jnp.logical_and(home, k == kk)
            pl.when(jnp.logical_not(own))(
                functools.partial(arrived, b_buf.at[kk, q], m_recv.at[kk, q], row, col)
            )
            pl.when(own)(pltpu.make_async_copy(t_buf.at[kk, q], b_buf.at[kk, q], loc_sem.at[q]).wait)

        @pl.loop(0, 8, unroll=4)
        def _(p):
            pos = q * 8 + p
            ii = pair_index(pos)
            b0 = b_buf[0, q, p].astype(F32)
            b1 = b_buf[1, q, p].astype(F32)
            mirrored = (
                jnp.where(low, b0, b1),
                pltpu.roll(jnp.where(low, b1, b0), 64, 1),
            )
            grads = []
            for h in range(2):
                i = ii + 32 * h
                sym = own_buf[i].astype(F32) + mirrored[h]
                top = jnp.max(sym, axis=0, keepdims=True)
                ex = jnp.exp(sym - top)
                prob = ex / jnp.sum(ex, axis=0, keepdims=True)
                tgt = tgt_ref[pl.ds(i, 1), :]
                hot = jnp.where(level == tgt, 1.0, 0.0)
                grad = 2.0 * (prob - hot)
                g_buf[i] = dot_nn(grad.T.astype(BF), wdt).astype(BF)
                grads.append(grad.astype(BF))
            gt_buf[p] = dot_nn(wd, jnp.concatenate(grads, axis=1)).astype(BF)

        @pl.loop(0, 8, unroll=2)
        def _(p):
            pos = q * 8 + p
            block, m = pos // 4, pos % 4
            gt = gt_buf[p]
            for side, w in ((0, wec), (1, wo_ref)):
                for n in range(4):
                    u = dot_nn(w[pl.ds(n * 256, 256), :], gt).astype(BF)
                    for h in range(2):
                        base = pl.multiple_of((m % 2) * 128 + (m // 2) * 32 + 64 * h, 32)
                        for f in range(8):
                            e = n * 8 + f
                            xs[side, block, pl.ds(base, 32), e * 128 : (e + 1) * 128] = u[
                                f * 32 : (f + 1) * 32, h * 128 : (h + 1) * 128
                            ]

        for lo in range(4):
            rows = pl.ds(lo * 16 + 4 * q, 4)
            cp = pltpu.make_async_copy(g_buf.at[rows], g_hbm.at[rows], out_sem.at[q, lo])
            cp.start()
            out_copies.append(cp)
        if q == 1:
            pass_on(left, right, (1, 2, 5, 6), (2, 3))
        if q == 2:
            pass_on(flip_left, flip_right, (3, 4, 7, 8), (4, 5))

    for side, r, slot in ((0, far, 5), (1, far, 6), (0, flip_far, 7), (1, flip_far, 8)):
        gather_wait(r, slot, side)
    share(far, 6)
    share(flip_far, 7)
    for slot, r in enumerate((row, flip, left, right, flip_left, flip_right, far, flip_far)):
        r = r + 1 - 2 * k
        arrived(whole(r), p_recv.at[slot], row, col)

    other = (1 - yl) * 4
    home4 = pl.multiple_of(yl * 4, 4)

    def contract(block):
        for side in range(2):
            out = dot_nt(lrg[1 - side], xs[side, block])
            for half in range(2):
                o32[...] = out[:, half * 128 : (half + 1) * 128]
                for w in range(16):
                    part[block, w // 2, side, half, (w % 2) * 16 : (w % 2) * 16 + 16, :] = o32[
                        pl.ds(w, 16, stride=16), :
                    ].astype(BF)
        if BLOCK_Y[block]:
            go(
                remote(
                    part.at[block, pl.ds(other, 4)], got_y.at[block], y_send.at[block], y_recv.at[block],
                    row, other + z,
                )
            )
        else:
            for d in range(1, 4):
                zz = (z + d) % 4
                for y2 in range(2):
                    go(
                        remote(
                            part.at[block, y2 * 4 + zz], got_z.at[block, d - 1, y2],
                            z_send.at[block, d - 1, y2], z_recv.at[block, d - 1, y2], row, yl * 4 + zz,
                        )
                    )

    def second(block):
        if BLOCK_Y[block]:
            arrived(got_y.at[block], y_recv.at[block], row, col)

            @pl.loop(0, 4)
            def _(zz):
                for side in range(2):
                    for half in range(2):
                        part[block, home4 + zz, side, half] = (
                            part[block, home4 + zz, side, half].astype(F32)
                            + got_y[block, zz, side, half].astype(F32)
                        ).astype(BF)

            for d in range(1, 4):
                zz = (z + d) % 4
                go(
                    remote(
                        part.at[block, yl * 4 + zz], got_z.at[block, d - 1, 0],
                        z_send.at[block, d - 1, 0], z_recv.at[block, d - 1, 0], row, yl * 4 + zz,
                    )
                )
        else:
            for d in range(1, 4):
                for y2 in range(2):
                    arrived(got_z.at[block, d - 1, y2], z_recv.at[block, d - 1, y2], row, col)
            for y2 in range(2):
                for side in range(2):
                    for half in range(2):
                        total = part[block, y2 * 4 + z, side, half].astype(F32)
                        for d in range(3):
                            total += got_z[block, d, y2, side, half].astype(F32)
                        part[block, y2 * 4 + z, side, half] = total.astype(BF)
            go(
                remote(
                    part.at[block, other + z], got_y.at[block, 0], y_send.at[block], y_recv.at[block],
                    row, other + z,
                )
            )

    def third(block):
        if BLOCK_Y[block]:
            for d in range(1, 4):
                arrived(got_z.at[block, d - 1, 0], z_recv.at[block, d - 1, 0], row, col)
        else:
            arrived(got_y.at[block, 0], y_recv.at[block], row, col)
        for side in range(2):
            for half in range(2):
                total = part[block, col, side, half].astype(F32)
                if BLOCK_Y[block]:
                    for d in range(3):
                        total += got_z[block, d, 0, side, half].astype(F32)
                else:
                    total += got_y[block, 0, side, half].astype(F32)
                tile = side * 16 + block * 2 + half
                for t in range(2):
                    fin32[pl.ds(t * 32 + tile, 16, stride=64), :] = total[t * 16 : (t + 1) * 16]

    for block in range(8):
        contract(block)
        if block >= 2:
            second(block - 2)
        if block >= 5:
            third(block - 5)
    second(6)
    second(7)
    for block in range(3, 8):
        third(block)

    for there in range(16):
        fin16[there] = fin32[pl.ds(there * 64, 64), :].astype(BF)
    fin_ref[row] = fin16[row]
    for step in range(1, 16):
        there = (row + step) % 16
        go(remote(fin16.at[there], fin_ref.at[row], f_send.at[step], f_recv.at[step], there, col))
    for step in range(1, 16):
        source = (row - step + 16) % 16
        arrived(fin_ref.at[source], f_recv.at[step], row, col)
    for cp, when in sends:
        if when is None:
            cp.wait_send()
        else:
            pl.when(when)(cp.wait_send)
    for cp in out_copies:
        cp.wait()


def main(a, tgt, wd, bias, wo, lhs, rhs):
    dma = pltpu.SemaphoreType.DMA
    return pl.pallas_call(
        main_kernel,
        out_shape=(
            jax.ShapeDtypeStruct((64, 128, 128), BF),
            jax.ShapeDtypeStruct((16, 64, 128), BF),
        ),
        in_specs=[VM] * 7,
        out_specs=(pl.BlockSpec(memory_space=pl.ANY), VM),
        scratch_shapes=[
            pltpu.VMEM((8192, 128), F32),
            pltpu.VMEM((2, 4, 8, 64, 128), BF),
            pltpu.VMEM((2, 4, 8, 64, 128), BF),
            pltpu.VMEM((2, 2, 8, 64, 128), BF),
            pltpu.VMEM((3, 2, 2, 8, 64, 128), BF),
            pltpu.VMEM((512, 128), F32),
            pltpu.VMEM((2, 256, 4096), BF),
            pltpu.VMEM((64, 128, 128), BF),
            pltpu.VMEM((1024, 128), F32),
            pltpu.VMEM((1024, 128), BF),
            pltpu.VMEM((2, 8, 256, 4096), BF),
            pltpu.VMEM((256, 128), F32),
            pltpu.VMEM((8, 8, 2, 2, 32, 128), BF),
            pltpu.VMEM((8, 4, 2, 2, 32, 128), BF),
            pltpu.VMEM((8, 3, 2, 2, 2, 32, 128), BF),
            pltpu.VMEM((1024, 128), F32),
            pltpu.VMEM((16, 64, 128), BF),
            pltpu.VMEM((64, 64, 128), BF),
            pltpu.VMEM((8, 128, 256), BF),
            dma((4,)),
            dma((2, 4)),
            dma((2, 4)),
            dma((2, 2)),
            dma((2, 2)),
            dma((3, 2, 2)),
            dma((3, 2, 2)),
            dma((9,)),
            dma((9,)),
            dma((8,)),
            dma((8,)),
            dma((4, 4)),
            dma((8,)),
            dma((8,)),
            dma((8, 3, 2)),
            dma((8, 3, 2)),
            dma((16,)),
            dma((16,)),
        ],
        compiler_params=pltpu.CompilerParams(
            collective_id=0, has_side_effects=True, vmem_limit_bytes=67043328
        ),
        name="main",
    )(a, tgt, wd, bias, wo, lhs, rhs)


def norm_forward(v):
    centered = v - jnp.mean(v, axis=0, keepdims=True)
    inv = lax.rsqrt(jnp.mean(centered * centered, axis=0, keepdims=True) + 1e-05)
    return centered * inv, inv


def norm_backward(g, normed, inv):
    first = jnp.mean(g, axis=0, keepdims=True)
    second = jnp.mean(g * normed, axis=0, keepdims=True)
    return inv * (g - first - normed * second)


def column(ref):
    return jnp.broadcast_to(ref[...], (128, ref.shape[1])).T[:, :1]


def tail_kernel(
    g_in, fin_ref, side_ref, arrive_ref, lw_ref, rw_ref, og_ref, tg_ref, gw_ref, uw_ref, dw_ref, g_out, out_ref,
    wts, g_stage, g_sem,
):
    fetch = [
        pltpu.make_async_copy(g_in.at[pl.ds(n * 16, 16)], g_stage.at[pl.ds(n * 16, 16)], g_sem.at[0, n])
        for n in range(4)
    ]
    store = [
        pltpu.make_async_copy(g_stage.at[pl.ds(n * 16, 16)], g_out.at[pl.ds(n * 16, 16)], g_sem.at[1, n])
        for n in range(4)
    ]
    for cp in fetch:
        cp.start()
    for cp, back in zip(fetch, store):
        cp.wait()
        back.start()
    lanes = 256
    gwt = gw_ref[...].astype(F32).T.astype(BF)
    uwt = uw_ref[...].astype(F32).T.astype(BF)
    dwt = dw_ref[...]
    gw, uw, dw = gw_ref[...], uw_ref[...], dwt.astype(F32).T.astype(BF)
    lwt, rwt = lw_ref[...], rw_ref[...]
    ab = jnp.concatenate([lwt] * 4 + [rwt] * 4, axis=0).astype(F32).T.astype(BF)
    og, tg = column(og_ref), column(tg_ref)
    group = lax.broadcasted_iota(jnp.int32, (16, 128), 1) // 32
    zero = jnp.zeros((16, 128), BF)

    @pl.loop(0, 2)
    def _(s):
        @pl.loop(0, 1024 // lanes)
        def _(n):
            for r in range(lanes // 64):
                for side in range(2):
                    rows = fin_ref[n * (lanes // 64) + r, pl.ds(pl.multiple_of(s * 32 + side * 16, 16), 16), :]
                    for lo in range(4):
                        wts[pl.ds(r * 64 + lo * 16, 16), side * 128 : side * 128 + 128] = jnp.where(
                            group == lo, rows, zero
                        )
            at = pl.ds(pl.multiple_of(n * lanes, lanes), lanes)
            ng = (dot_nt(ab, wts[...]) * (1.0 / 256)).astype(BF).astype(F32)
            v = side_ref[s, :, at].astype(F32)
            n1, inv1 = norm_forward(v)
            nin = (n1 * tg).astype(BF)
            gate = dot_nn(gwt, nin)
            up = dot_nn(uwt, nin)
            sig = jax.nn.sigmoid(gate)
            act = gate * sig
            hidden = (act * up).astype(BF)
            n2, inv2 = norm_forward(v + dot_nn(dwt, hidden))
            mid = arrive_ref[s, :, at].astype(F32) + norm_backward(ng * og, n2, inv2)
            hg = dot_nn(dw, mid.astype(BF))
            gg = (hg * up * sig * (1.0 + gate * (1.0 - sig))).astype(BF)
            ug = (hg * act).astype(BF)
            nrg = dot_nn(gw, gg) + dot_nn(uw, ug)
            out_ref[s, :, at] = (mid + norm_backward(nrg * tg, n1, inv1)).astype(BF)

    for cp in store:
        cp.wait()


def tail(g, fin, side, arrive, lw, rw, og, tg, gw, uw, dw):
    hbm = pl.BlockSpec(memory_space=pl.ANY)
    return pl.pallas_call(
        tail_kernel,
        out_shape=(
            jax.ShapeDtypeStruct((64, 128, 128), BF),
            jax.ShapeDtypeStruct((2, 64, 1024), BF),
        ),
        in_specs=[hbm] + [VM] * 10,
        out_specs=(hbm, VM),
        scratch_shapes=[
            pltpu.VMEM((256, 256), BF),
            pltpu.VMEM((64, 128, 128), BF),
            pltpu.SemaphoreType.DMA((2, 4)),
        ],
        compiler_params=pltpu.CompilerParams(vmem_limit_bytes=67043328),
        name="tail",
    )(g, fin, side, arrive, lw, rw, og, tg, gw, uw, dw)


def per_device(
    pair_activation, target_distance_bins, distogram_weight, distogram_bias, outer_pair_weight,
    stored_lhs_operand, stored_rhs_operand, left_projection_weight, right_projection_weight,
    outer_mean_norm_gain, transition_norm_gain, gate_weight, up_weight, down_weight,
    side_stack_entry, arriving_stack_derivative,
):
    g, fin = main(
        pair_activation, target_distance_bins, distogram_weight.T, distogram_bias.reshape(1, -1),
        outer_pair_weight, stored_lhs_operand, stored_rhs_operand,
    )
    g, out = tail(
        g, fin, side_stack_entry, arriving_stack_derivative, left_projection_weight.T,
        right_projection_weight.T, outer_mean_norm_gain.reshape(1, -1),
        transition_norm_gain.reshape(1, -1), gate_weight, up_weight, down_weight.T,
    )
    return g, out


def solution(mesh):
    return jax.shard_map(
        per_device,
        mesh=mesh,
        in_specs=(
            P("row", "col", None),
            P("row", "col"),
            P(),
            P(),
            P(),
            P("row", None, "col"),
            P("row", None, "col"),
            P(),
            P(),
            P(),
            P(),
            P(),
            P(),
            P(),
            P(("row", "col"), None, None),
            P(("row", "col"), None, None),
        ),
        out_specs=(P("row", "col", None), P(("row", "col"), None, None)),
        check_vma=False,
    )
```

time: 186 us -> 122 us (0.66)
  the two profiles are of different devices: /device:TPU:97 before, /device:TPU:1 now
where the time goes in v2:
time: 122 us
  Pallas kernels  121 us (99%)
    pallas_call x1, Pallas kernels, main(): pl.pallas_call(main_kernel, out_shape=(jax.ShapeDtypeStruct((64, 128, 128...  110 us
    pallas_call x1, Pallas kernels, tail(): pl.pallas_call(tail_kernel, out_shape=(jax.ShapeDtypeStruct((64, 128, 128...  11 us

profile of v2, /device:TPU:1, one launch (start us, length us, event | category | flops | bytes accessed | tf_op | source)
XLA Modules:
  0.0 122.1 jit_solution(9556714937879348745)
XLA Ops:
  0.6 110.3 %main.1 = (bf16[64,128,128]{2,1,0:T(8,128)(2,1)}, bf16[16,64,128]{2,1,0:T(8,128)(2,1)}) custom-call(bf16[64,128,128]{2,1,0:T(8,128)(2,1)} %a_ref.1, s32[64,128]{1,0:T(8,128)} %tgt_ref.1, bf16[64,128]{1,0:T(8,128)(2,1)} %bitcast.8, f32[1,64]{1,0:T(1,128)} %bitcast.11, bf16[1024,128]{1,0:T(8,128)(2,1)} %wo_ref.1, bf16[16,32,128]{2,1,0:T(8,128)(2,1)} %lhs_ref.1, ...), custom_call_target="tpu_custom_call" | custom-call | tf_op jit(solution)/shard_map/main/pallas_call | solution.py:404
  110.9 11.0 %tail.1 = (bf16[64,128,128]{2,1,0:T(8,128)(2,1)}, bf16[2,64,1024]{2,1,0:T(8,128)(2,1)}) custom-call(bf16[64,128,128]{2,1,0:T(8,128)(2,1)} %get-tuple-element.4.g_in, bf16[16,64,128]{2,1,0:T(8,128)(2,1)} %get-tuple-element.5.fin_ref, bf16[2,64,1024]{2,1,0:T(8,128)(2,1)} %side_ref.1, bf16[2,64,1024]{2,1,0:T(8,128)(2,1)} %arrive_ref.1, bf16[32,64]{1,0:T(8,128)(2,1)} %bitcast.9, ...), custom_call_target="tpu_custom_call" | custom-call | tf_op jit(solution)/shard_map/tail/pallas_call | solution.py:537

commit v3 on v2

v3 whole, which is shorter than its diff:
```python
import functools

import jax
import jax.numpy as jnp
from jax import lax
from jax.experimental import pallas as pl
from jax.experimental.pallas import tpu as pltpu
from jax.sharding import PartitionSpec as P

MESH = pl.DeviceIdType.MESH
BF = jnp.bfloat16
F32 = jnp.float32
VM = pl.BlockSpec(memory_space=pltpu.VMEM)


def dot_nt(a, b):
    return lax.dot_general(a, b, (((1,), (1,)), ((), ())), preferred_element_type=F32)


def dot_nn(a, b):
    return lax.dot_general(a, b, (((1,), (0,)), ((), ())), preferred_element_type=F32)


def place():
    row, col = lax.axis_index("row"), lax.axis_index("col")
    return row, col, row // 8, (row // 2) % 4, row % 2, col // 4, col % 4


def greet_all(row, col):
    barrier = pltpu.get_barrier_semaphore()
    me = row * 8 + col

    def greet(step, _):
        other = (me + step) % 128
        pl.semaphore_signal(
            barrier, inc=1, device_id={"row": other // 8, "col": other % 8}, device_id_type=MESH
        )
        return 0

    lax.fori_loop(1, 128, greet, 0)
    return barrier


def remote(src, dst, send, recv, row, col):
    return pltpu.make_async_remote_copy(
        src, dst, send, recv, device_id={"row": row, "col": col}, device_id_type=MESH
    )


def pair_index(pos):
    block, m = pos // 4, pos % 4
    return 2 * block + m % 2 + 16 * (m // 2)


def bias_columns(bias_ref):
    return jnp.broadcast_to(bias_ref[...], (128, 64)).T


def arrived(dst, recv, row, col):
    remote(dst, dst, recv, recv, row, col).wait_recv()


def norm_forward(v):
    centered = v - jnp.mean(v, axis=0, keepdims=True)
    inv = lax.rsqrt(jnp.mean(centered * centered, axis=0, keepdims=True) + 1e-05)
    return centered * inv, inv


def norm_backward(g, normed, inv):
    first = jnp.mean(g, axis=0, keepdims=True)
    second = jnp.mean(g * normed, axis=0, keepdims=True)
    return inv * (g - first - normed * second)


def column(ref):
    return jnp.broadcast_to(ref[...], (128, ref.shape[1])).T[:, :1]


UNITS = ((True, (0, 1)), (False, (2, 3)), (True, (4, 5)), (False, (6,)), (True, (7,)))
SCHEDULE = (
    (0, 0), (0, 1), (0, 2), (0, 3), (1, 0), (0, 4), (1, 1), (1, 2), (1, 3), (2, 0), (1, 4), (2, 1), (2, 2), (2, 3), (2, 4)
)


def main_kernel(
    a_hbm, tgt_ref, wd_ref, bias_ref, wo_ref, lhs_ref, rhs_ref, side_hbm, arrive_hbm, lw_ref, rw_ref, og_ref,
    tg_ref, gw_ref, uw_ref, dw_ref, g_hbm, out_ref, a_ref, side_ref, arrive_ref, fin_ref, n2_buf, inv_buf, wts, de_buf, a32, t_buf, b_buf, ra_buf, rb_buf, s32, lrg, g_buf, w32, wec, xs, o32, fin32, fin16, own_buf, gt_buf,
    *rest,
):
    n_units = len(UNITS)
    parts, gots_y, gots_z = rest[:n_units], rest[n_units : 2 * n_units], rest[2 * n_units : 3 * n_units]
    (
    de_send, de_recv, in_sem, loc_sem, m_send, m_recv, ra_send, ra_recv, rb_send, rb_recv,
    gx_send, gx_recv, p_send, p_recv, out_sem, y_send, y_recv, z_send, z_recv, f_send, f_recv,
    ) = rest[3 * n_units :]
    row, col, yh, x, k, yl, z = place()
    chip = row // 2
    diag = x == z
    same_y = yh == yl
    home = jnp.logical_and(diag, same_y)
    partner = row + 1 - 2 * k
    sends = []

    def go(cp, when=None):
        if when is None:
            cp.start()
        else:
            pl.when(when)(cp.start)
        sends.append((cp, when))

    def block_rows(r):
        return pl.ds(pl.multiple_of(r * 16, 16), 16)

    def x_row(r, d):
        return (r // 8) * 8 + (((r // 2) % 4 + d) % 4) * 2 + r % 2

    barrier = greet_all(row, col)
    loads = [
        pltpu.make_async_copy(a_hbm.at[pl.ds(n * 16, 16)], a_ref.at[pl.ds(n * 16, 16)], in_sem.at[n])
        for n in range(4)
    ]
    loads.append(pltpu.make_async_copy(side_hbm, side_ref, in_sem.at[4]))
    loads.append(pltpu.make_async_copy(arrive_hbm, arrive_ref, in_sem.at[5]))
    for cp in loads:
        cp.start()
    mine = block_rows(row)
    for side, ref in ((0, lhs_ref), (1, rhs_ref)):
        for s in range(16):
            s32[pl.ds(s * 32, 32), :] = ref[s].astype(F32)
        for e in range(32):
            lrg[side, mine, e * 128 : (e + 1) * 128] = s32[pl.ds(e, 16, stride=32), :].astype(BF)

    def whole(r):
        return lrg.at[:, block_rows(r)]

    def share(r, slot):
        go(remote(whole(r), whole(r), p_send.at[slot], p_recv.at[slot], partner, col))

    def gather_send(r, slot, there):
        go(pass_copy(r, slot, there))

    def pass_copy(r, slot, there):
        return remote(whole(r), whole(r), gx_send.at[slot], gx_recv.at[slot], there, col)

    def gather_wait(r, slot):
        arrived(whole(r), gx_recv.at[slot], row, col)

    flip = (row + 8) % 16
    left, right = x_row(row, 3), x_row(row, 1)
    flip_left, flip_right = x_row(flip, 3), x_row(flip, 1)
    far, flip_far = x_row(row, 2), x_row(flip, 2)
    wdt = wd_ref[...]
    wd = wdt.astype(F32).T.astype(BF)
    bias = bias_columns(bias_ref)

    for n in range(4):
        loads[n].wait()

        @pl.loop(0, 16, unroll=4)
        def _(p):
            i = n * 16 + p
            a32[pl.ds(pl.multiple_of(i * 128, 128), 128), :] = a_ref[i].astype(F32)

    for q in range(4):
        for kk in range(2):

            @pl.loop(0, 8, unroll=8)
            def _(p):
                ii = pair_index(q * 8 + p) + 64 * kk
                first = a32[pl.ds(ii + 32 * k, 64, stride=128), :]
                second = a32[pl.ds(ii + 32 * (1 - k), 64, stride=128), :]
                both = jnp.concatenate([first, second], axis=0).astype(BF)
                t_buf[kk, q, p] = (dot_nt(wdt, both) + bias).astype(BF)

            if q == 0 and kk == 0:
                pl.semaphore_wait(barrier, 127)
                gather_send(row, 0, flip)
                gather_send(row, 1, right)
                gather_send(row, 2, left)
                share(row, 0)
            src = t_buf.at[kk, q]
            final = remote(src, b_buf.at[k, q], m_send.at[kk, q], m_recv.at[k, q], 2 * col + kk, chip)
            local = pltpu.make_async_copy(src, b_buf.at[k, q], loc_sem.at[q])
            own = jnp.logical_and(home, k == kk)
            if q % 2 == 0:
                direct = jnp.logical_and(jnp.logical_or(diag, same_y), jnp.logical_not(own))
                if q == 0:
                    hop = remote(
                        src, ra_buf.at[kk, 0], m_send.at[kk, q], ra_recv.at[kk, 0],
                        yl * 8 + x * 2 + k, yh * 4 + z,
                    )
                else:
                    hop = remote(
                        src, de_buf.at[0, kk], m_send.at[kk, q], de_recv.at[0, kk],
                        yh * 8 + x * 2 + k, (1 - yl) * 4 + z,
                    )
            else:
                direct = jnp.logical_and(diag, jnp.logical_not(own))
                slot = (z - x + 3) % 4
                hop = remote(
                    src, rb_buf.at[slot, kk, q // 2], m_send.at[kk, q], rb_recv.at[slot, kk, q // 2],
                    yl * 8 + x * 2 + k, yh * 4 + x,
                )
            relayed = jnp.logical_not(jnp.logical_or(direct, own))
            pl.when(own)(local.start)
            pl.when(direct)(final.start)
            pl.when(relayed)(hop.start)
            sends.append((final, jnp.logical_not(own)))

    w32[...] = wo_ref[...].astype(F32)
    for e in range(32):
        wec[pl.ds(e * 32, 32), :] = w32[pl.ds(e, 32, stride=32), :].astype(BF)

    gather_wait(flip, 0)
    gather_send(flip, 3, right)
    gather_send(flip, 4, left)
    share(flip, 1)

    upward = z % 2 == 1

    def pass_on(near_left, near_right, slots, shares):
        gather_wait(near_left, slots[0])
        go(pass_copy(near_left, slots[2], right), upward)
        share(near_left, shares[0])
        gather_wait(near_right, slots[1])
        go(pass_copy(near_right, slots[2], left), jnp.logical_not(upward))
        share(near_right, shares[1])

    relay_a = jnp.logical_not(jnp.logical_or(diag, same_y))

    carrier = jnp.logical_and(same_y, jnp.logical_not(diag))

    def detour(leg):
        for kk in range(2):
            pl.when(carrier)(functools.partial(arrived, de_buf.at[leg, kk], de_recv.at[leg, kk], row, col))
            if leg == 0:
                dst, recv = de_buf.at[1, kk], de_recv.at[1, kk]
                there = ((1 - yh) * 8 + x * 2 + k, (1 - yl) * 4 + z)
            else:
                dst, recv = ra_buf.at[kk, 1], ra_recv.at[kk, 1]
                there = (yh * 8 + x * 2 + k, (1 - yl) * 4 + z)
            go(remote(de_buf.at[leg, kk], dst, de_send.at[leg, kk], recv, *there), carrier)

    def relay(j):
        for kk in range(2):
            pl.when(relay_a)(functools.partial(arrived, ra_buf.at[kk, j], ra_recv.at[kk, j], row, col))
            go(
                remote(
                    ra_buf.at[kk, j], b_buf.at[k, 2 * j], ra_send.at[kk, j], m_recv.at[k, 2 * j],
                    2 * (yh * 4 + z) + kk, yl * 4 + x,
                ),
                relay_a,
            )
        for kk in range(2):
            for slot in range(3):
                zs = (x + 1 + slot) % 4
                pl.when(diag)(
                    functools.partial(arrived, rb_buf.at[slot, kk, j], rb_recv.at[slot, kk, j], row, col)
                )
                go(
                    remote(
                        rb_buf.at[slot, kk, j], b_buf.at[k, 2 * j + 1], rb_send.at[slot, kk, j],
                        m_recv.at[k, 2 * j + 1], 2 * (yh * 4 + zs) + kk, yl * 4 + x,
                    ),
                    diag,
                )

    @pl.loop(0, 64, unroll=8)
    def _(i):
        own_buf[i] = (dot_nt(wdt, a_ref[i]) + bias).astype(BF)

    relay(0)
    pass_on(left, right, (1, 2, 5), (2, 3))
    detour(0)
    for cp in loads[4:]:
        cp.wait()
    gw, uw, dwt = gw_ref[...], uw_ref[...], dw_ref[...]
    gwt, uwt = gw.astype(F32).T.astype(BF), uw.astype(F32).T.astype(BF)
    og, tg = column(og_ref), column(tg_ref)

    def keep(s, n, which):
        base = ((s * 4 + n) * 2 + which) * 512
        return [pl.ds(pl.multiple_of(base + 256 * t, 256), 256) for t in range(2)]

    def transition(s):
        @pl.loop(0, 4)
        def _(n):
            at = pl.ds(pl.multiple_of(n * 256, 256), 256)
            v = side_ref[s, :, at].astype(F32)
            n1, _ = norm_forward(v)
            nin = (n1 * tg).astype(BF)
            gate, up = dot_nn(gwt, nin), dot_nn(uwt, nin)
            hidden = (gate * jax.nn.sigmoid(gate) * up).astype(BF)
            n2, inv2 = norm_forward(v + dot_nn(dwt, hidden))
            n2_buf[s, :, at] = n2
            inv_buf[s, :, at] = jnp.broadcast_to(inv2, (8, 256))
            for which, value in ((0, gate), (1, up)):
                for t, rows in enumerate(keep(s, n, which)):
                    a32[rows, :] = value[:, t * 128 : (t + 1) * 128]

    transition(0)
    detour(1)
    pass_on(flip_left, flip_right, (3, 4, 6), (4, 5))
    relay(1)
    transition(1)

    lane = lax.broadcasted_iota(jnp.int32, (64, 128), 1)
    level = lax.broadcasted_iota(jnp.int32, (64, 128), 0)
    low = lane < 64
    out_copies = []
    for q in range(4):
        for kk in range(2):
            own = jnp.logical_and(home, k == kk)
            pl.when(jnp.logical_not(own))(
                functools.partial(arrived, b_buf.at[kk, q], m_recv.at[kk, q], row, col)
            )
            pl.when(own)(pltpu.make_async_copy(t_buf.at[kk, q], b_buf.at[kk, q], loc_sem.at[q]).wait)

        @pl.loop(0, 8, unroll=4)
        def _(p):
            pos = q * 8 + p
            ii = pair_index(pos)
            b0 = b_buf[0, q, p].astype(F32)
            b1 = b_buf[1, q, p].astype(F32)
            mirrored = (
                jnp.where(low, b0, b1),
                pltpu.roll(jnp.where(low, b1, b0), 64, 1),
            )
            grads = []
            for h in range(2):
                i = ii + 32 * h
                sym = own_buf[i].astype(F32) + mirrored[h]
                top = jnp.max(sym, axis=0, keepdims=True)
                ex = jnp.exp(sym - top)
                prob = ex / jnp.sum(ex, axis=0, keepdims=True)
                tgt = tgt_ref[pl.ds(i, 1), :]
                hot = jnp.where(level == tgt, 1.0, 0.0)
                grad = 2.0 * (prob - hot)
                g_buf[i] = dot_nn(grad.T.astype(BF), wdt).astype(BF)
                grads.append(grad.astype(BF))
            gt_buf[p] = dot_nn(wd, jnp.concatenate(grads, axis=1)).astype(BF)

        @pl.loop(0, 8, unroll=2)
        def _(p):
            pos = q * 8 + p
            block, m = pos // 4, pos % 4
            gt = gt_buf[p]
            for side, w in ((0, wec), (1, wo_ref)):
                for n in range(4):
                    u = dot_nn(w[pl.ds(n * 256, 256), :], gt).astype(BF)
                    for h in range(2):
                        base = pl.multiple_of((m % 2) * 128 + (m // 2) * 32 + 64 * h, 32)
                        for f in range(8):
                            e = n * 8 + f
                            xs[side, block, pl.ds(base, 32), e * 128 : (e + 1) * 128] = u[
                                f * 32 : (f + 1) * 32, h * 128 : (h + 1) * 128
                            ]

        for lo in range(4):
            rows = pl.ds(lo * 16 + 4 * q, 4)
            cp = pltpu.make_async_copy(g_buf.at[rows], g_hbm.at[rows], out_sem.at[q, lo])
            cp.start()
            out_copies.append(cp)

    gather_wait(far, 5)
    share(far, 6)
    gather_wait(flip_far, 6)
    share(flip_far, 7)
    for slot, r in enumerate((row, flip, left, right, flip_left, flip_right, far, flip_far)):
        r = r + 1 - 2 * k
        arrived(whole(r), p_recv.at[slot], row, col)

    other = 1 - yl

    def contract(u):
        y_first, blocks = UNITS[u]
        part = parts[u]
        for n, block in enumerate(blocks):
            for side in range(2):
                out = dot_nt(lrg[1 - side], xs[side, block])
                for half in range(2):
                    o32[...] = out[:, half * 128 : (half + 1) * 128]
                    for w in range(16):
                        y2, z2 = w // 8, (w // 2) % 4
                        at = (y2, z2) if y_first else (z2, y2)
                        part[at[0], at[1], n, side, half, (w % 2) * 16 : (w % 2) * 16 + 16, :] = o32[
                            pl.ds(w, 16, stride=16), :
                        ].astype(BF)
        if y_first:
            go(remote(part.at[other], gots_y[u], y_send.at[u], y_recv.at[u], row, other * 4 + z))
        else:
            for d in range(1, 4):
                zz = (z + d) % 4
                go(remote(part.at[zz], gots_z[u].at[d - 1], z_send.at[u, d - 1], z_recv.at[u, d - 1], row, yl * 4 + zz))

    def tiles(u):
        return [(n, side, half) for n in range(len(UNITS[u][1])) for side in range(2) for half in range(2)]

    def second(u):
        part = parts[u]
        if UNITS[u][0]:
            arrived(gots_y[u], y_recv.at[u], row, col)
            for z2 in range(4):
                for at in tiles(u):
                    part[(yl, z2) + at] = (part[(yl, z2) + at].astype(F32) + gots_y[u][(z2,) + at].astype(F32)).astype(BF)
            for d in range(1, 4):
                zz = (z + d) % 4
                go(
                    remote(
                        part.at[yl, zz], gots_z[u].at[d - 1], z_send.at[u, d - 1], z_recv.at[u, d - 1],
                        row, yl * 4 + zz,
                    )
                )
        else:
            for d in range(1, 4):
                arrived(gots_z[u].at[d - 1], z_recv.at[u, d - 1], row, col)
            for y2 in range(2):
                for at in tiles(u):
                    total = part[(z, y2) + at].astype(F32)
                    for d in range(3):
                        total += gots_z[u][(d, y2) + at].astype(F32)
                    part[(z, y2) + at] = total.astype(BF)
            go(remote(part.at[z, other], gots_y[u], y_send.at[u], y_recv.at[u], row, other * 4 + z))

    def third(u):
        y_first, blocks = UNITS[u]
        if y_first:
            for d in range(1, 4):
                arrived(gots_z[u].at[d - 1], z_recv.at[u, d - 1], row, col)
        else:
            arrived(gots_y[u], y_recv.at[u], row, col)
        for at in tiles(u):
            if y_first:
                total = parts[u][(yl, z) + at].astype(F32)
                for d in range(3):
                    total += gots_z[u][(d,) + at].astype(F32)
            else:
                total = parts[u][(z, yl) + at].astype(F32) + gots_y[u][at].astype(F32)
            n, side, half = at
            tile = side * 16 + blocks[n] * 2 + half
            for t in range(2):
                fin32[pl.ds(t * 32 + tile, 16, stride=64), :] = total[t * 16 : (t + 1) * 16]

    for stage, u in SCHEDULE:
        (contract, second, third)[stage](u)

    for there in range(16):
        fin16[there] = fin32[pl.ds(there * 64, 64), :].astype(BF)
    fin_ref[row] = fin16[row]
    for step in range(1, 16):
        there = (row + step) % 16
        go(remote(fin16.at[there], fin_ref.at[row], f_send.at[step], f_recv.at[step], there, col))
    for step in range(1, 16):
        source = (row - step + 16) % 16
        arrived(fin_ref.at[source], f_recv.at[step], row, col)
    dw = dwt.astype(F32).T.astype(BF)
    ab = jnp.concatenate([lw_ref[...]] * 4 + [rw_ref[...]] * 4, axis=0).astype(F32).T.astype(BF)
    group = lax.broadcasted_iota(jnp.int32, (16, 128), 1) // 32
    zero = jnp.zeros((16, 128), BF)

    @pl.loop(0, 2)
    def _(s):
        @pl.loop(0, 4)
        def _(n):
            for r in range(4):
                for side in range(2):
                    rows = fin_ref[n * 4 + r, pl.ds(pl.multiple_of(s * 32 + side * 16, 16), 16), :]
                    for lo in range(4):
                        wts[pl.ds(r * 64 + lo * 16, 16), side * 128 : side * 128 + 128] = jnp.where(
                            group == lo, rows, zero
                        )
            at = pl.ds(pl.multiple_of(n * 256, 256), 256)
            ng = (dot_nt(ab, wts[...]) * (1.0 / 256)).astype(BF).astype(F32)
            mid = arrive_ref[s, :, at].astype(F32) + norm_backward(ng * og, n2_buf[s, :, at], inv_buf[s, :1, at])
            hg = dot_nn(dw, mid.astype(BF))
            gate, up = [
                jnp.concatenate([a32[rows, :] for rows in keep(s, n, which)], axis=1) for which in range(2)
            ]
            sig = jax.nn.sigmoid(gate)
            act = gate * sig
            gg = (hg * up * sig * (1.0 + gate * (1.0 - sig))).astype(BF)
            ug = (hg * act).astype(BF)
            nrg = dot_nn(gw, gg) + dot_nn(uw, ug)
            n1, inv1 = norm_forward(side_ref[s, :, at].astype(F32))
            out_ref[s, :, at] = (mid + norm_backward(nrg * tg, n1, inv1)).astype(BF)

    for cp, when in sends:
        if when is None:
            cp.wait_send()
        else:
            pl.when(when)(cp.wait_send)
    for cp in out_copies:
        cp.wait()


def main(*args):
    dma = pltpu.SemaphoreType.DMA
    hbm = pl.BlockSpec(memory_space=pl.ANY)
    return pl.pallas_call(
        main_kernel,
        out_shape=(
            jax.ShapeDtypeStruct((64, 128, 128), BF),
            jax.ShapeDtypeStruct((2, 64, 1024), BF),
        ),
        in_specs=[hbm] + [VM] * 6 + [hbm, hbm] + [VM] * 7,
        out_specs=(hbm, VM),
        scratch_shapes=[
            pltpu.VMEM((64, 128, 128), BF),
            pltpu.VMEM((2, 64, 1024), BF),
            pltpu.VMEM((2, 64, 1024), BF),
            pltpu.VMEM((16, 64, 128), BF),
            pltpu.VMEM((2, 64, 1024), F32),
            pltpu.VMEM((2, 8, 1024), F32),
            pltpu.VMEM((256, 256), BF),
            pltpu.VMEM((2, 2, 8, 64, 128), BF),
            pltpu.VMEM((8192, 128), F32),
            pltpu.VMEM((2, 4, 8, 64, 128), BF),
            pltpu.VMEM((2, 4, 8, 64, 128), BF),
            pltpu.VMEM((2, 2, 8, 64, 128), BF),
            pltpu.VMEM((3, 2, 2, 8, 64, 128), BF),
            pltpu.VMEM((512, 128), F32),
            pltpu.VMEM((2, 256, 4096), BF),
            pltpu.VMEM((64, 128, 128), BF),
            pltpu.VMEM((1024, 128), F32),
            pltpu.VMEM((1024, 128), BF),
            pltpu.VMEM((2, 8, 256, 4096), BF),
            pltpu.VMEM((256, 128), F32),
            pltpu.VMEM((1024, 128), F32),
            pltpu.VMEM((16, 64, 128), BF),
            pltpu.VMEM((64, 64, 128), BF),
            pltpu.VMEM((8, 128, 256), BF),
            *[pltpu.VMEM(((2, 4) if y else (4, 2)) + (len(b), 2, 2, 32, 128), BF) for y, b in UNITS],
            *[pltpu.VMEM(((4,) if y else ()) + (len(b), 2, 2, 32, 128), BF) for y, b in UNITS],
            *[pltpu.VMEM(((3,) if y else (3, 2)) + (len(b), 2, 2, 32, 128), BF) for y, b in UNITS],
            dma((2, 2)),
            dma((2, 2)),
            dma((6,)),
            dma((4,)),
            dma((2, 4)),
            dma((2, 4)),
            dma((2, 2)),
            dma((2, 2)),
            dma((3, 2, 2)),
            dma((3, 2, 2)),
            dma((9,)),
            dma((9,)),
            dma((8,)),
            dma((8,)),
            dma((4, 4)),
            dma((8,)),
            dma((8,)),
            dma((8, 3)),
            dma((8, 3)),
            dma((16,)),
            dma((16,)),
        ],
        compiler_params=pltpu.CompilerParams(
            collective_id=0, has_side_effects=True, vmem_limit_bytes=67043328
        ),
        name="main",
    )(*args)


def hand_on_kernel(g_in, o_in, g_out, o_out, g_stage, o_stage, sem):
    pairs = [(g_in.at[pl.ds(n * 8, 8)], g_stage.at[pl.ds(n * 8, 8)], g_out.at[pl.ds(n * 8, 8)]) for n in range(8)]
    pairs.append((o_in, o_stage, o_out))
    fetch = [pltpu.make_async_copy(a, b, sem.at[0, n]) for n, (a, b, _) in enumerate(pairs)]
    store = [pltpu.make_async_copy(b, c, sem.at[1, n]) for n, (_, b, c) in enumerate(pairs)]
    for cp in fetch:
        cp.start()
    for cp, back in zip(fetch, store):
        cp.wait()
        back.start()
    for back in store:
        back.wait()


def hand_on(g, out):
    hbm = pl.BlockSpec(memory_space=pl.ANY)
    return pl.pallas_call(
        hand_on_kernel,
        out_shape=(jax.ShapeDtypeStruct(g.shape, g.dtype), jax.ShapeDtypeStruct(out.shape, out.dtype)),
        in_specs=[hbm, hbm],
        out_specs=(hbm, hbm),
        scratch_shapes=[pltpu.VMEM(g.shape, BF), pltpu.VMEM(out.shape, BF), pltpu.SemaphoreType.DMA((2, 9))],
        compiler_params=pltpu.CompilerParams(vmem_limit_bytes=67043328),
        name="hand_on",
    )(g, out)


def per_device(
    pair_activation, target_distance_bins, distogram_weight, distogram_bias, outer_pair_weight,
    stored_lhs_operand, stored_rhs_operand, left_projection_weight, right_projection_weight,
    outer_mean_norm_gain, transition_norm_gain, gate_weight, up_weight, down_weight,
    side_stack_entry, arriving_stack_derivative,
):
    g, out = main(
        pair_activation, target_distance_bins, distogram_weight.T, distogram_bias.reshape(1, -1),
        outer_pair_weight, stored_lhs_operand, stored_rhs_operand, side_stack_entry,
        arriving_stack_derivative, left_projection_weight.T, right_projection_weight.T,
        outer_mean_norm_gain.reshape(1, -1), transition_norm_gain.reshape(1, -1), gate_weight, up_weight,
        down_weight.T,
    )
    return hand_on(g, out)


def solution(mesh):
    return jax.shard_map(
        per_device,
        mesh=mesh,
        in_specs=(
            P("row", "col", None),
            P("row", "col"),
            P(),
            P(),
            P(),
            P("row", None, "col"),
            P("row", None, "col"),
            P(),
            P(),
            P(),
            P(),
            P(),
            P(),
            P(),
            P(("row", "col"), None, None),
            P(("row", "col"), None, None),
        ),
        out_specs=(P("row", "col", None), P(("row", "col"), None, None)),
        check_vma=False,
    )
```

time: 122 us -> 112 us (0.918)
  Pallas kernels: 121 us -> 111 us
    pallas_call x1, Pallas kernels: 11 us -> 2.5 us  [hand_on(): pl.pallas_call(hand_on_kernel, out_shape=(jax.ShapeDtypeStruct(g.shape, g...]
    pallas_call x1, Pallas kernels: 110 us -> 109 us  [main(): pl.pallas_call(main_kernel, out_shape=(jax.ShapeDtypeStruct((64, 128, 128...]
where the time goes in v3:
time: 112 us
  Pallas kernels  111 us (99%)
    pallas_call x1, Pallas kernels, main(): pl.pallas_call(main_kernel, out_shape=(jax.ShapeDtypeStruct((64, 128, 128...  109 us
    pallas_call x1, Pallas kernels, hand_on(): pl.pallas_call(hand_on_kernel, out_shape=(jax.ShapeDtypeStruct(g.shape, g...  2.5 us

profile of v3, /device:TPU:1, one launch (start us, length us, event | category | flops | bytes accessed | tf_op | source)
XLA Modules:
  0.0 112.3 jit_solution(17697114457681853753)
XLA Ops:
  0.6 109.0 %main.1 = (bf16[64,128,128]{2,1,0:T(8,128)(2,1)}, bf16[2,64,1024]{2,1,0:T(8,128)(2,1)}) custom-call(bf16[64,128,128]{2,1,0:T(8,128)(2,1)} %a_hbm.1, s32[64,128]{1,0:T(8,128)} %tgt_ref.1, bf16[64,128]{1,0:T(8,128)(2,1)} %bitcast.8, f32[1,64]{1,0:T(1,128)} %bitcast.11, bf16[1024,128]{1,0:T(8,128)(2,1)} %wo_ref.1, bf16[16,32,128]{2,1,0:T(8,128)(2,1)} %lhs_ref.1, ...), custom_call_target="tpu_custom_call" | custom-call | tf_op jit(solution)/shard_map/main/pallas_call | solution.py:499
  109.6 2.5 %hand_on.1 = (bf16[64,128,128]{2,1,0:T(8,128)(2,1)}, bf16[2,64,1024]{2,1,0:T(8,128)(2,1)}) custom-call(bf16[64,128,128]{2,1,0:T(8,128)(2,1)} %get-tuple-element.4.g_in, bf16[2,64,1024]{2,1,0:T(8,128)(2,1)} %get-tuple-element.5.o_in), custom_call_target="tpu_custom_call" | custom-call | tf_op jit(solution)/shard_map/hand_on/pallas_call | solution.py:580

commit v4 on v3

--- a/solution.py
+++ b/solution.py
@@ -300,7 +300,6 @@
 
     transition(0)
     detour(1)
-    pass_on(flip_left, flip_right, (3, 4, 6), (4, 5))
     relay(1)
     transition(1)
 
@@ -361,6 +360,8 @@
             cp = pltpu.make_async_copy(g_buf.at[rows], g_hbm.at[rows], out_sem.at[q, lo])
             cp.start()
             out_copies.append(cp)
+        if q == 0:
+            pass_on(flip_left, flip_right, (3, 4, 6), (4, 5))
 
     gather_wait(far, 5)
     share(far, 6)
@@ -460,17 +461,17 @@
 
     @pl.loop(0, 2)
     def _(s):
-        @pl.loop(0, 4)
+        @pl.loop(0, 4, unroll=4)
         def _(n):
             for r in range(4):
                 for side in range(2):
                     rows = fin_ref[n * 4 + r, pl.ds(pl.multiple_of(s * 32 + side * 16, 16), 16), :]
                     for lo in range(4):
-                        wts[pl.ds(r * 64 + lo * 16, 16), side * 128 : side * 128 + 128] = jnp.where(
+                        wts[n, pl.ds(r * 64 + lo * 16, 16), side * 128 : side * 128 + 128] = jnp.where(
                             group == lo, rows, zero
                         )
             at = pl.ds(pl.multiple_of(n * 256, 256), 256)
-            ng = (dot_nt(ab, wts[...]) * (1.0 / 256)).astype(BF).astype(F32)
+            ng = (dot_nt(ab, wts[n]) * (1.0 / 256)).astype(BF).astype(F32)
             mid = arrive_ref[s, :, at].astype(F32) + norm_backward(ng * og, n2_buf[s, :, at], inv_buf[s, :1, at])
             hg = dot_nn(dw, mid.astype(BF))
             gate, up = [
@@ -511,7 +512,7 @@
             pltpu.VMEM((16, 64, 128), BF),
             pltpu.VMEM((2, 64, 1024), F32),
             pltpu.VMEM((2, 8, 1024), F32),
-            pltpu.VMEM((256, 256), BF),
+            pltpu.VMEM((4, 256, 256), BF),
             pltpu.VMEM((2, 2, 8, 64, 128), BF),
             pltpu.VMEM((8192, 128), F32),
             pltpu.VMEM((2, 4, 8, 64, 128), BF),

time: 112 us -> 110 us (0.982)
  Pallas kernels: 111 us -> 109 us
    pallas_call x1, Pallas kernels: 109 us -> 107 us  [main(): pl.pallas_call(main_kernel, out_shape=(jax.ShapeDtypeStruct((64, 128, 128...]
where the time goes in v4:
time: 110 us
  Pallas kernels  109 us (99%)
    pallas_call x1, Pallas kernels, main(): pl.pallas_call(main_kernel, out_shape=(jax.ShapeDtypeStruct((64, 128, 128...  107 us
    pallas_call x1, Pallas kernels, hand_on(): pl.pallas_call(hand_on_kernel, out_shape=(jax.ShapeDtypeStruct(g.shape, g...  2.5 us

profile of v4, /device:TPU:1, one launch (start us, length us, event | category | flops | bytes accessed | tf_op | source)
XLA Modules:
  0.0 110.2 jit_solution(11806870416515808956)
XLA Ops:
  0.6 106.9 %main.1 = (bf16[64,128,128]{2,1,0:T(8,128)(2,1)}, bf16[2,64,1024]{2,1,0:T(8,128)(2,1)}) custom-call(bf16[64,128,128]{2,1,0:T(8,128)(2,1)} %a_hbm.1, s32[64,128]{1,0:T(8,128)} %tgt_ref.1, bf16[64,128]{1,0:T(8,128)(2,1)} %bitcast.8, f32[1,64]{1,0:T(1,128)} %bitcast.11, bf16[1024,128]{1,0:T(8,128)(2,1)} %wo_ref.1, bf16[16,32,128]{2,1,0:T(8,128)(2,1)} %lhs_ref.1, ...), custom_call_target="tpu_custom_call" | custom-call | tf_op jit(solution)/shard_map/main/pallas_call | solution.py:500
  107.6 2.5 %hand_on.1 = (bf16[64,128,128]{2,1,0:T(8,128)(2,1)}, bf16[2,64,1024]{2,1,0:T(8,128)(2,1)}) custom-call(bf16[64,128,128]{2,1,0:T(8,128)(2,1)} %get-tuple-element.4.g_in, bf16[2,64,1024]{2,1,0:T(8,128)(2,1)} %get-tuple-element.5.o_in), custom_call_target="tpu_custom_call" | custom-call | tf_op jit(solution)/shard_map/hand_on/pallas_call | solution.py:581
